TPU v7x, 256 devices: a whole 4x4x8 slice. The times are simulated.
256 devices in a mesh: rows: 32 (over y, x, core), outs: 8 (over z).
Axes of the slice: x: 4, y: 4, z: 8, core: 2. Of those that a mesh axis runs over, the one named last changes fastest.
Arguments:
- codes: int32 [49152, 256], P('rows'), may hold values from 0 to 31
- node_of_row: int32 [49152], P('rows'), may hold values from 0 to 15
- grad: bfloat16 [49152, 128], P('rows', 'outs'), may hold values from -6 to 6
- hess: bfloat16 [49152, 128], P('rows', 'outs'), may hold values from 0.099609375 to 1
- small_side: int32 [8], replicated, may hold values from 0 to 1
- evicted: int32 [8], replicated, may hold values from 0 to 1, as said below
- parent_hist: float32 [2, 8, 128, 8192], P(None, None, 'outs', 'rows'), as said below
Outputs:
- node_hist: float32 [2, 16, 128, 8192], P(None, None, 'outs', 'rows')
- split_gain: float32 [16, 8192], P(None, 'rows')
- best_gain: float32 [16], replicated
Inputs may be any that keep to these rules, and one draw needn't show every extreme that they name: `evicted`: exactly 3 of the 8 entries are 1. `parent_hist`: the hessian component is not negative.
All inputs are finite; a program needn't handle non-finite values.
Results may differ from a plain program's by a relative error of at most 0.0003.
Values may be sent and summed in bfloat16 or wider, within the bound.
A program may use at most 256 MiB of HBM per device.

v0:
```python
import jax
import jax.numpy as jnp
from jax import lax
from jax.sharding import PartitionSpec as P

BINS = 32
TARGETS = 128


def slot_values(grads, hesses, nodes, slots):
    count = grads.shape[0]
    hit = (nodes[:, None] == slots[None, :])[:, :, None]
    grad_part = jnp.where(hit, grads[:, None, :], jnp.zeros((), grads.dtype))
    hess_part = jnp.where(hit, hesses[:, None, :], jnp.zeros((), hesses.dtype))
    return jnp.concatenate([grad_part.reshape(count, -1), hess_part.reshape(count, -1)], axis=1)


def contract(block, values):
    count = block.shape[0]
    onehot = block[:, :, None] == jnp.arange(BINS, dtype=jnp.int32)[None, None, :]
    onehot = onehot.reshape(count, -1).astype(jnp.bfloat16)
    return lax.dot_general(
        onehot, values, (((0,), (0,)), ((), ())), preferred_element_type=jnp.float32
    )


def gain_terms(node_hist):
    grads = node_hist[0]
    hesses = node_hist[1]
    nodes, targets, span = grads.shape
    grads = grads.reshape(nodes, targets, span // BINS, BINS)
    hesses = hesses.reshape(nodes, targets, span // BINS, BINS)
    left_g = jnp.cumsum(grads, axis=3)
    left_h = jnp.cumsum(hesses, axis=3)
    total_g = left_g[..., -1:]
    total_h = left_h[..., -1:]

    def score(a, s):
        return a * a / (jnp.maximum(s, 0.0) + 1.0)

    gain = (
        score(left_g, left_h) + score(total_g - left_g, total_h - left_h) - score(total_g, total_h)
    )
    return jnp.sum(gain, axis=1).reshape(nodes, span)


def local(codes, node_of_row, grad, hess, small_side, evicted, parent_hist):
    pairs = small_side.shape[0]
    local_targets = grad.shape[1]
    slots = jnp.arange(2 * pairs, dtype=jnp.int32)
    slot_count = slots.shape[0]
    span = codes.shape[1] // lax.axis_size("rows") * BINS
    values = slot_values(grad, hess, node_of_row, slots)
    built = lax.psum_scatter(contract(codes, values), "rows", scatter_dimension=0, tiled=True)
    built = jnp.transpose(built.reshape(span, 2, slot_count, local_targets), (1, 2, 3, 0))
    small = (small_side == 0)[None, :, None, None]
    pair_view = built.reshape(2, pairs, 2, local_targets, span)
    child = jnp.where(small, pair_view[:, :, 0], pair_view[:, :, 1])
    rebuilt = jnp.where(small, pair_view[:, :, 1], pair_view[:, :, 0])
    gone = (evicted == 1)[None, :, None, None]
    sibling = jnp.where(gone, rebuilt, parent_hist - child)
    first = jnp.where(small, child, sibling)
    second = jnp.where(small, sibling, child)
    node_hist = jnp.stack([first, second], axis=2).reshape(2, 2 * pairs, local_targets, span)
    partial_gain = gain_terms(node_hist)
    split_gain = lax.psum(partial_gain, "outs") / TARGETS
    best_gain = lax.pmax(jnp.max(split_gain, axis=1), "rows")
    return (node_hist, split_gain, best_gain)


def solution(mesh):
    return jax.shard_map(
        local,
        mesh=mesh,
        in_specs=(
            P("rows", None),
            P("rows"),
            P("rows", "outs"),
            P("rows", "outs"),
            P(),
            P(),
            P(None, None, "outs", "rows"),
        ),
        out_specs=(P(None, None, "outs", "rows"), P(None, "rows"), P()),
        check_vma=False,
    )
```

profile of v0, /device:TPU:1, one launch (start us, length us, event | category | flops | bytes accessed | tf_op | source)
XLA Modules:
  0.0 378.4 jit_solution(12323342735052473486)
XLA Ops:
  7.2 0.0 copy-start.3
  7.2 0.0 copy-start.2
  7.2 0.0 reduce-scatter.2.cloned.1.call-start
  7.2 0.7 iota_compare_fusion
  7.9 3.0 copy.36
  11.0 0.1 eq.47
  11.1 11.0 %bitcast_compare_fusion = pred[1536,8192]{0,1:T(32,128)(4,1)S(1)} fusion(s32[8192]{0:T(1024)S(1)} %eq.47, s32[1536,256]{0,1:T(8,128)} %copy.36), kind=kLoop, calls=%fused_computation | loop fusion | flops 12582912 | bytes 14188544 | tf_op jit(solution)/shard_map/eq | solution.py:20
  22.1 0.0 copy-done.3
  22.1 0.0 copy-done.2
  22.1 1.3 broadcast_select_fusion.1
  23.4 18.1 %fusion = f32[8192,512]{1,0:T(8,128)} fusion(pred[1536,8192]{0,1:T(32,128)(4,1)S(1)} %bitcast_compare_fusion, bf16[1536,256]{0,1:T(8,128)(2,1)} %bitcast.57, bf16[1536,256]{0,1:T(8,128)(2,1)} %bitcast.56), kind=kOutput, calls=%fused_computation.1 | convolution fusion | flops 12888047616 | bytes 30932992 | tf_op jit(solution)/shard_map/dot_general | solution.py:22
  41.5 0.0 copy-start.4
  41.5 0.0 copy-start.5
  41.5 0.0 copy-start.1
  41.5 0.0 reduce-scatter.2.cloned.1.call-update
  41.5 0.6 copy-done.4
  42.1 0.0 copy-done.5
  42.2 125.0 %reduce-scatter.2.cloned.1.call-done = f32[256,512]{1,0:T(8,128)} async-done(((f32[8192,512]{1,0:T(8,128)}), f32[256,512]{1,0:T(8,128)}) %reduce-scatter.2.cloned.1.call-update) | async-done | bytes 524304 | tf_op jit(solution)/shard_map/reduce_scatter | solution.py:54
  167.1 1.2 copy.37
  168.4 0.0 copy-done.1
  168.4 0.1 select_bitcast_fusion.1
  168.5 0.0 copy-start
  168.6 0.6 copy-done
  169.3 0.3 reshape_squeeze.6
  169.5 47.2 %reduce_window_sum.17 = f32[16,16,8,32]{3,2,1,0:T(8,128)S(1)} reduce-window(f32[16,16,8,32]{3,2,1,0:T(8,128)S(1)} %reshape_squeeze.6, f32[]{:T(128)} %constant.10.clone.1), window={size=1x1x1x32 pad=0_0x0_0x0_0x31_0}, to_apply=%region_1.2 | reduce-window | flops 2031616 | bytes 524292 | tf_op jit(solution)/shard_map/jit(cumsum)/reduce_window_sum | solution.py:33
  216.7 0.3 slice.34
  217.0 1.4 copy.48
  218.5 1.6 copy.50
  220.1 0.3 reshape_squeeze.7
  220.4 47.2 %reduce_window_sum.18 = f32[16,16,8,32]{3,2,1,0:T(8,128)S(1)} reduce-window(f32[16,16,8,32]{3,2,1,0:T(8,128)S(1)} %reshape_squeeze.7, f32[]{:T(128)} %constant.10.clone.1), window={size=1x1x1x32 pad=0_0x0_0x0_0x31_0}, to_apply=%region_2.3 | reduce-window | flops 2031616 | bytes 524292 | tf_op jit(solution)/shard_map/jit(cumsum)/reduce_window_sum | solution.py:34
  267.5 0.3 slice.35
  267.9 1.4 copy.49
  269.3 2.2 copy.51
  271.5 1.0 pad_maximum_fusion
  272.5 0.9 divide_bitcast_fusion
  273.4 0.1 copy.46
  273.5 1.8 subtract_reduce_fusion
  275.3 0.1 reshape.64
  275.4 22.7 %psum.7 = f32[16,256]{1,0:T(8,128)S(1)} all-reduce(f32[16,256]{1,0:T(8,128)S(1)} %reshape.64), channel_id=1, replica_groups=mesh['rows'=32,'outs'=8] {'outs'}, use_global_device_ids=true, to_apply=%region_4.5 | all-reduce | flops 4096 | bytes 32768 | tf_op jit(solution)/shard_map/psum | solution.py:66
  298.1 0.7 fusion.8
  298.8 71.9 %pmax.7 = f32[16]{0:T(128)} all-reduce(f32[16]{0:T(128)S(1)} %get-tuple-element.3), channel_id=1, replica_groups=mesh['rows'=32,'outs'=8] {'rows'}, use_global_device_ids=true, to_apply=%region_6.7 | all-reduce | flops 16 | bytes 128 | tf_op jit(solution)/shard_map/pmax | solution.py:67
  370.7 0.8 copy.39
  (5 shorter events, 0.1 us)
Async XLA Ops:
  7.2 14.9 %copy-start.3 = (bf16[1536,16]{0,1:T(8,128)(2,1)S(1)}, bf16[1536,16]{0,1:T(8,128)(2,1)}, u32[]{:S(2)}) copy-start(bf16[1536,16]{0,1:T(8,128)(2,1)} %param.10) | copy-start | bytes 147460
  7.2 14.9 %copy-start.2 = (bf16[1536,16]{0,1:T(8,128)(2,1)S(1)}, bf16[1536,16]{0,1:T(8,128)(2,1)}, u32[]{:S(2)}) copy-start(bf16[1536,16]{0,1:T(8,128)(2,1)} %param.9) | copy-start | bytes 147460
  7.2 160.0 %reduce-scatter.2.cloned.1.call-start = ((), (), s32[]{:S(2)}) async-start(), calls=%async_computation.1 | async-start | bytes 17301504 | tf_op jit(solution)/shard_map/reduce_scatter | solution.py:54
  41.5 0.7 copy-start.4
  41.5 0.7 copy-start.5
  41.5 126.9 %copy-start.1 = (f32[2,8,16,256]{3,2,1,0:T(8,128)S(1)}, f32[2,8,16,256]{3,2,1,0:T(8,128)}, u32[]{:S(2)}) copy-start(f32[2,8,16,256]{3,2,1,0:T(8,128)} %param.13) | copy-start | bytes 786436
  168.5 0.7 copy-start
Sparse Core Ops, SparseCore 0:
  41.6 125.4 reduce-scatter.1
where the time goes:
time: 379 us; the launch traced here: 378 us
  waiting for transfers between devices  125 us (33%)
  other arithmetic  112 us (30%)
  blocking collectives  94.6 us (25%)
  matrix products  18.1 us (5%)
  local copies, waits for them, and re-layouts  14.6 us (4%)
  between operations  14.2 us (4%)
    reduce_scatter x1, waiting for transfers between devices, local(): lax.psum_scatter(contract(codes, values), 'rows', scatter_dimension=0, ti...  125 us
    pmax x1, blocking collectives, local(): best_gain = lax.pmax(jnp.max(split_gain, axis=1), 'rows')  71.9 us
    another operation x1, other arithmetic, gain_terms(): left_g = jnp.cumsum(grads, axis=3)  47.2 us
    another operation x1, other arithmetic, gain_terms(): left_h = jnp.cumsum(hesses, axis=3)  47.2 us
    psum x1, blocking collectives, local(): split_gain = lax.psum(partial_gain, 'outs') / TARGETS  22.7 us
    dot_general x1, matrix products, contract(): lax.dot_general(onehot, values, (((0,), (0,)), ((), ())), preferred_eleme...  18.1 us
    eq x1, other arithmetic, contract(): block[:, :, None] == jnp.arange(BINS, dtype=jnp.int32)[None, None, :]  11 us
  transfers between devices with their start and end apart: 1, of which 1 were waited for; matrix products, arithmetic and copies ran while one was open for 0% of the time, Pallas kernels for 0%

commit v1 on v0

v1 whole, which is shorter than its diff:
```python
import functools

import jax
import jax.numpy as jnp
import numpy as np
from jax import lax
from jax.experimental import pallas as pl
from jax.experimental.pallas import tpu as pltpu
from jax.sharding import PartitionSpec as P

BINS = 32
ROW_TILE = 2048


def hist_kernel(codes_ref, v_ref, node_ref, out_ref, *, nodes):
    @pl.when(pl.program_id(0) == 0)
    def _():
        out_ref[...] = jnp.zeros_like(out_ref)

    feats, rows = codes_ref.shape
    one = jnp.ones((), jnp.bfloat16)
    zero = jnp.zeros((), jnp.bfloat16)
    bins = lax.broadcasted_iota(jnp.int32, (BINS, rows), 0)
    onehot = jnp.concatenate(
        [jnp.where(codes_ref[f : f + 1, :] == bins, one, zero) for f in range(feats)], axis=0
    )
    node = node_ref[...]
    v = v_ref[...]
    tl = v.shape[0] // 2
    blocks = []
    for c in range(2):
        vc = v[c * tl : (c + 1) * tl]
        for n in range(nodes):
            blocks.append(jnp.where(node == n, vc, zero))
    vals = jnp.concatenate(blocks, axis=0)
    out_ref[...] += lax.dot_general(
        vals, onehot, (((1,), (1,)), ((), ())), preferred_element_type=jnp.float32
    )


def build_hist(codes_t, v_t, node_all, nodes):
    feats, total = codes_t.shape
    width = v_t.shape[0]
    tile = min(ROW_TILE, total)
    steps = total // tile
    out_rows = width * nodes
    cols = feats * BINS
    return pl.pallas_call(
        functools.partial(hist_kernel, nodes=nodes),
        out_shape=jax.ShapeDtypeStruct((out_rows, cols), jnp.float32),
        grid=(steps,),
        in_specs=[
            pl.BlockSpec((feats, tile), lambda i: (0, i)),
            pl.BlockSpec((width, tile), lambda i: (0, i)),
            pl.BlockSpec((1, tile), lambda i: (0, i)),
        ],
        out_specs=pl.BlockSpec((out_rows, cols), lambda i: (0, 0)),
        cost_estimate=pl.CostEstimate(
            flops=2 * out_rows * cols * total,
            bytes_accessed=total * (feats * 4 + width * 2 + 4) + out_rows * cols * 4,
            transcendentals=0,
        ),
    )(codes_t, v_t, node_all)


def prefix_matrices(span):
    i = np.arange(span)[:, None]
    j = np.arange(span)[None, :]
    same = (i // BINS) == (j // BINS)
    tri = (same & (i <= j)).astype(np.float32)
    last = (i == (j // BINS) * BINS + BINS - 1).astype(np.float32)
    return jnp.asarray(tri), jnp.asarray(last)


def gain_terms(node_hist):
    _, nodes, targets, span = node_hist.shape
    tri, last = prefix_matrices(span)
    flat = node_hist.reshape(2 * nodes * targets, span)
    left = jnp.dot(flat, tri, precision=lax.Precision.HIGHEST, preferred_element_type=jnp.float32)
    total = jnp.dot(left, last, precision=lax.Precision.HIGHEST, preferred_element_type=jnp.float32)
    left = left.reshape(2, nodes, targets, span)
    total = total.reshape(2, nodes, targets, span)
    left_g, left_h = left[0], left[1]
    total_g, total_h = total[0], total[1]

    def score(a, s):
        return a * a / (jnp.maximum(s, 0.0) + 1.0)

    gain = (
        score(left_g, left_h) + score(total_g - left_g, total_h - left_h) - score(total_g, total_h)
    )
    return jnp.sum(gain, axis=1)


def local(codes, node_of_row, grad, hess, small_side, evicted, parent_hist):
    pairs = small_side.shape[0]
    nodes = 2 * pairs
    local_targets = grad.shape[1]
    targets = local_targets * lax.axis_size("outs")
    codes_t = lax.all_to_all(
        codes.astype(jnp.int16).T, "rows", 0, 1, tiled=True
    ).astype(jnp.int32)
    v_t = lax.all_gather(jnp.concatenate([grad.T, hess.T], axis=0), "rows", axis=1, tiled=True)
    node_all = lax.all_gather(node_of_row.reshape(1, -1), "rows", axis=1, tiled=True)
    span = codes_t.shape[0] * BINS
    built = build_hist(codes_t, v_t, node_all, nodes).reshape(2, nodes, local_targets, span)
    small = (small_side == 0)[None, :, None, None]
    pair_view = built.reshape(2, pairs, 2, local_targets, span)
    child = jnp.where(small, pair_view[:, :, 0], pair_view[:, :, 1])
    rebuilt = jnp.where(small, pair_view[:, :, 1], pair_view[:, :, 0])
    gone = (evicted == 1)[None, :, None, None]
    sibling = jnp.where(gone, rebuilt, parent_hist - child)
    first = jnp.where(small, child, sibling)
    second = jnp.where(small, sibling, child)
    node_hist = jnp.stack([first, second], axis=2).reshape(2, nodes, local_targets, span)
    partial_gain = gain_terms(node_hist)
    split_gain = lax.psum(partial_gain, "outs") / targets
    best_gain = lax.pmax(jnp.max(split_gain, axis=1), "rows")
    return (node_hist, split_gain, best_gain)


def solution(mesh):
    return jax.shard_map(
        local,
        mesh=mesh,
        in_specs=(
            P("rows", None),
            P("rows"),
            P("rows", "outs"),
            P("rows", "outs"),
            P(),
            P(),
            P(None, None, "outs", "rows"),
        ),
        out_specs=(P(None, None, "outs", "rows"), P(None, "rows"), P()),
        check_vma=False,
    )
```

time: 379 us -> 194 us (0.51)
  waiting for transfers between devices: 125 us -> 12.9 us
  other arithmetic: 112 us -> 6 us
  blocking collectives: 94.6 us -> 126 us
  Pallas kernels: 0 us -> 22.3 us
  matrix products: 18.1 us -> 1.16 us
  local copies, waits for them, and re-layouts: 14.6 us -> 1.92 us
  starting transfers between devices: 0.04 us -> 8.63 us
    reduce_scatter x1 -> x0, waiting for transfers between devices: 125 us -> none  [local(): lax.psum_scatter(contract(codes, values), 'rows', scatter_dimension=0, ti...]
    another operation x5 -> x2, other arithmetic: 95.5 us -> 1.26 us  [local(): jnp.stack([first, second], axis=2).reshape(2, nodes, local_targets, span)]
    all_gather x0 -> x1, blocking collectives: none -> 33.2 us  [local(): lax.all_gather(node_of_row.reshape(1, -1), 'rows', axis=1, tiled=True)]
    pallas_call x0 -> x1, Pallas kernels: none -> 22.3 us  [build_hist(): pl.pallas_call(functools.partial(hist_kernel, nodes=nodes), out_shape=jax...]
    dot_general x1 -> x2, matrix products: 18.1 us -> 1.16 us  [the longest x1 0.58 us: gain_terms(): jnp.dot(left, last, precision=lax.Precision.HIGHEST, preferred_element_ty...]
    all_gather x0 -> x1, waiting for transfers between devices: none -> 12.9 us  [local(): lax.all_gather(jnp.concatenate([grad.T, hess.T], axis=0), 'rows', axis=1,...]
    eq x2 -> x0, other arithmetic: 11.7 us -> none  [the longest x1 11 us: contract(): block[:, :, None] == jnp.arange(BINS, dtype=jnp.int32)[None, None, :]]
    all_to_all x0 -> x1, starting transfers between devices: none -> 8.59 us  [local(): lax.all_to_all(codes.astype(jnp.int16).T, 'rows', 0, 1, tiled=True)]
  transfers between devices with their start and end apart: 1 -> 2, of which waited for: 1 -> 1; matrix products, arithmetic and copies ran while one was open for 0% -> 2% of each run, Pallas kernels for 0% -> 0%
where the time goes in v1:
time: 194 us; the launch traced here: 193 us
  blocking collectives  126 us (65%)
  Pallas kernels  22.3 us (11%)
  between operations  14.2 us (7%)
  waiting for transfers between devices  12.9 us (7%)
  starting transfers between devices  8.63 us (4%)
  other arithmetic  6 us (3%)
    pmax x1, blocking collectives, local(): best_gain = lax.pmax(jnp.max(split_gain, axis=1), 'rows')  69.9 us
    all_gather x1, blocking collectives, local(): lax.all_gather(node_of_row.reshape(1, -1), 'rows', axis=1, tiled=True)  33.2 us
    psum x1, blocking collectives, local(): split_gain = lax.psum(partial_gain, 'outs') / targets  23.1 us
    pallas_call x1, Pallas kernels, build_hist(): pl.pallas_call(functools.partial(hist_kernel, nodes=nodes), out_shape=jax...  22.3 us
    all_gather x1, waiting for transfers between devices, local(): lax.all_gather(jnp.concatenate([grad.T, hess.T], axis=0), 'rows', axis=1,...  12.9 us
    all_to_all x1, starting transfers between devices, local(): lax.all_to_all(codes.astype(jnp.int16).T, 'rows', 0, 1, tiled=True)  8.59 us
  transfers between devices with their start and end apart: 2, of which 1 were waited for; matrix products, arithmetic and copies ran while one was open for 2% of the time, Pallas kernels for 0%

profile of v1, /device:TPU:1, one launch (start us, length us, event | category | flops | bytes accessed | tf_op | source)
XLA Modules:
  0.0 193.3 jit_solution(1708288210358294601)
XLA Ops:
  7.2 0.0 all-gather.4.cloned.1.call-start
  7.2 1.5 pad_maximum_fusion.1
  8.7 0.0 all-gather.4.cloned.1.call-update
  8.7 1.9 copy.20
  10.6 0.0 copy-start.4
  10.6 0.0 copy-start.5
  10.6 0.0 copy-start.6
  10.6 1.0 convert_bitcast_fusion
  11.6 8.6 %all-to-all-start = ((s16[32,8,1536]{2,1,0:T(8,128)(2,1)}), s16[32,8,1536]{2,1,0:T(8,128)(2,1)S(1)}, u32[]{:S(2)}, u32[]{:S(2)}) async-start(s16[32,8,1536]{2,1,0:T(8,128)(2,1)} %convert_bitcast_fusion), calls=%async_computation | async-start | bytes 1572864 | tf_op jit(solution)/shard_map/all_to_all | solution.py:100
  20.2 0.0 copy-done.4
  20.2 33.2 %all-gather.1 = s32[32,1,1536]{2,1,0:T(1,128)} all-gather(s32[1,1,1536]{2,1,0:T(1,128)S(1)} %reshape.55), channel_id=2, replica_groups=mesh['rows'=32,'outs'=8] {'rows'}, dimensions={0}, use_global_device_ids=true | all-gather | bytes 202752 | tf_op jit(solution)/shard_map/all_gather | solution.py:104
  53.4 0.0 copy-done.5
  53.4 0.0 copy-done.6
  53.4 0.0 all-to-all-done
  53.4 1.4 convert_element_type.15
  54.8 12.9 %all-gather.4.cloned.1.call-done.v_ref = bf16[32,49152]{1,0:T(8,128)(2,1)} async-done(((bf16[32,1536]{1,0:T(8,128)(2,1)}), bf16[32,49152]{1,0:T(8,128)(2,1)}) %all-gather.4.cloned.1.call-update) | async-done | bytes 3145744 | tf_op jit(solution)/shard_map/all_gather | solution.py:103
  67.7 0.0 copy-start.3
  67.7 22.3 %shard_map.112 = f32[512,256]{1,0:T(8,128)} custom-call(s32[8,49152]{1,0:T(8,128)} %bitcast.59, bf16[32,49152]{1,0:T(8,128)(2,1)} %all-gather.4.cloned.1.call-done.v_ref, s32[1,49152]{1,0:T(1,128)} %bitcast.61), custom_call_target="tpu_custom_call" | custom-call | flops 12884901888 | bytes 5439488 | tf_op jit(solution)/shard_map/pallas_call | solution.py:48
  90.0 0.0 copy-start.1
  90.0 0.0 copy-done.3
  90.0 0.0 copy-start.2
  90.0 1.2 select_bitcast_fusion.1
  91.3 0.0 copy-start
  91.3 0.0 copy-done.1
  91.3 0.6 fusion.2
  91.9 0.0 copy-done.2
  91.9 0.6 fusion.3
  92.5 0.2 bitcast_reduce_fusion
  92.7 0.0 copy-done
  92.7 23.1 %psum.7 = f32[16,256]{1,0:T(8,128)S(1)} all-reduce(f32[16,256]{1,0:T(8,128)S(1)} %bitcast_reduce_fusion), channel_id=1, replica_groups=mesh['rows'=32,'outs'=8] {'outs'}, use_global_device_ids=true, to_apply=%region_1.2 | all-reduce | flops 4096 | bytes 32768 | tf_op jit(solution)/shard_map/psum | solution.py:117
  115.9 0.7 fusion.1
  116.6 69.9 %pmax.7 = f32[16]{0:T(128)} all-reduce(f32[16]{0:T(128)S(1)} %get-tuple-element.3), channel_id=1, replica_groups=mesh['rows'=32,'outs'=8] {'rows'}, use_global_device_ids=true, to_apply=%region_3.4 | all-reduce | flops 16 | bytes 128 | tf_op jit(solution)/shard_map/pmax | solution.py:118
  (3 shorter events, 0.0 us)
Async XLA Ops:
  7.2 60.5 %all-gather.4.cloned.1.call-start = ((), (), s32[]{:S(2)}) async-start(), calls=%async_computation.1 | async-start | bytes 3244032 | tf_op jit(solution)/shard_map/all_gather | solution.py:103
  10.6 9.6 %copy-start.4 = (s32[1536]{0:T(1024)S(1)}, s32[1536]{0:T(1024)}, u32[]{:S(2)}) copy-start(s32[1536]{0:T(1024)} %param.10) | copy-start | bytes 18436
  10.6 42.8 %copy-start.5 = (s32[8]{0:T(128)S(1)}, s32[8]{0:T(128)}, u32[]{:S(2)}) copy-start(s32[8]{0:T(128)} %param.14) | copy-start | bytes 100
  10.6 42.8 %copy-start.6 = (s32[8]{0:T(128)S(1)}, s32[8]{0:T(128)}, u32[]{:S(2)}) copy-start(s32[8]{0:T(128)} %param.13) | copy-start | bytes 100
  11.6 41.9 %all-to-all-start = ((s16[32,8,1536]{2,1,0:T(8,128)(2,1)}), s16[32,8,1536]{2,1,0:T(8,128)(2,1)S(1)}, u32[]{:S(2)}, u32[]{:S(2)}) async-start(s16[32,8,1536]{2,1,0:T(8,128)(2,1)} %convert_bitcast_fusion), calls=%async_computation | async-start | bytes 1572864 | tf_op jit(solution)/shard_map/all_to_all | solution.py:100
  67.7 22.3 %copy-start.3 = (f32[2,8,16,256]{3,2,1,0:T(8,128)S(1)}, f32[2,8,16,256]{3,2,1,0:T(8,128)}, u32[]{:S(2)}) copy-start(f32[2,8,16,256]{3,2,1,0:T(8,128)} %param.15) | copy-start | bytes 786436
  90.0 1.3 copy-start.1
  90.0 1.9 copy-start.2
  91.3 1.4 copy-start
Sparse Core Ops, SparseCore 0:
  11.2 56.4 all-gather.3

commit v2 on v1

--- a/solution.py
+++ b/solution.py
@@ -12,7 +12,7 @@
 ROW_TILE = 2048
 
 
-def hist_kernel(codes_ref, v_ref, node_ref, out_ref, *, nodes):
+def hist_kernel(codes_ref, v_ref, out_ref, *, nodes):
     @pl.when(pl.program_id(0) == 0)
     def _():
         out_ref[...] = jnp.zeros_like(out_ref)
@@ -24,26 +24,26 @@
     onehot = jnp.concatenate(
         [jnp.where(codes_ref[f : f + 1, :] == bins, one, zero) for f in range(feats)], axis=0
     )
-    node = node_ref[...]
     v = v_ref[...]
     tl = v.shape[0] // 2
+    node = v[2 * tl : 2 * tl + 1]
     blocks = []
     for c in range(2):
         vc = v[c * tl : (c + 1) * tl]
         for n in range(nodes):
-            blocks.append(jnp.where(node == n, vc, zero))
+            blocks.append(jnp.where(node == jnp.asarray(n, jnp.bfloat16), vc, zero))
     vals = jnp.concatenate(blocks, axis=0)
     out_ref[...] += lax.dot_general(
         vals, onehot, (((1,), (1,)), ((), ())), preferred_element_type=jnp.float32
     )
 
 
-def build_hist(codes_t, v_t, node_all, nodes):
+def build_hist(codes_t, v_t, nodes):
     feats, total = codes_t.shape
     width = v_t.shape[0]
     tile = min(ROW_TILE, total)
     steps = total // tile
-    out_rows = width * nodes
+    out_rows = (width - 1) * nodes
     cols = feats * BINS
     return pl.pallas_call(
         functools.partial(hist_kernel, nodes=nodes),
@@ -52,15 +52,14 @@
         in_specs=[
             pl.BlockSpec((feats, tile), lambda i: (0, i)),
             pl.BlockSpec((width, tile), lambda i: (0, i)),
-            pl.BlockSpec((1, tile), lambda i: (0, i)),
         ],
         out_specs=pl.BlockSpec((out_rows, cols), lambda i: (0, 0)),
         cost_estimate=pl.CostEstimate(
             flops=2 * out_rows * cols * total,
-            bytes_accessed=total * (feats * 4 + width * 2 + 4) + out_rows * cols * 4,
+            bytes_accessed=total * (feats * 4 + width * 2) + out_rows * cols * 4,
             transcendentals=0,
         ),
-    )(codes_t, v_t, node_all)
+    )(codes_t, v_t)
 
 
 def prefix_matrices(span):
@@ -92,6 +91,109 @@
     return jnp.sum(gain, axis=1)
 
 
+MESH_ID = pl.DeviceIdType.MESH
+
+
+def exchange_kernel(p_ref, split_ref, best_ref, gbuf, mbuf, gsend, grecv, msend, mrecv, *, targets):
+    n_rows = lax.axis_size("rows")
+    n_outs = lax.axis_size("outs")
+    r = lax.axis_index("rows")
+    o = lax.axis_index("outs")
+    barrier = pltpu.get_barrier_semaphore()
+    for k in range(1, n_outs):
+        pl.semaphore_signal(barrier, 1, device_id=(r, (o + k) % n_outs), device_id_type=MESH_ID)
+    for k in range(1, n_rows):
+        pl.semaphore_signal(barrier, 1, device_id=((r + k) % n_rows, o), device_id_type=MESH_ID)
+    pl.semaphore_wait(barrier, n_outs - 1 + n_rows - 1)
+
+    sends = []
+    for k in range(1, n_outs):
+        copy = pltpu.make_async_remote_copy(
+            src_ref=p_ref,
+            dst_ref=gbuf.at[o],
+            send_sem=gsend.at[k],
+            recv_sem=grecv.at[o],
+            device_id=(r, (o + k) % n_outs),
+            device_id_type=MESH_ID,
+        )
+        copy.start()
+        sends.append(copy)
+    gbuf[o] = p_ref[...]
+    for k in range(1, n_outs):
+        src = (o + n_outs - k) % n_outs
+        pltpu.make_async_remote_copy(
+            src_ref=p_ref,
+            dst_ref=gbuf.at[src],
+            send_sem=gsend.at[k],
+            recv_sem=grecv.at[src],
+            device_id=(r, src),
+            device_id_type=MESH_ID,
+        ).wait_recv()
+    for copy in sends:
+        copy.wait_send()
+    acc = gbuf[0]
+    for j in range(1, n_outs):
+        acc = acc + gbuf[j]
+    split = acc / targets
+    split_ref[...] = split
+    width = mbuf.shape[2]
+    mbuf[r] = jnp.broadcast_to(jnp.max(split, axis=1, keepdims=True), (split.shape[0], width))
+
+    sends = []
+    for k in range(1, n_rows):
+        copy = pltpu.make_async_remote_copy(
+            src_ref=mbuf.at[r],
+            dst_ref=mbuf.at[r],
+            send_sem=msend.at[k],
+            recv_sem=mrecv.at[r],
+            device_id=((r + k) % n_rows, o),
+            device_id_type=MESH_ID,
+        )
+        copy.start()
+        sends.append(copy)
+    for k in range(1, n_rows):
+        src = (r + n_rows - k) % n_rows
+        pltpu.make_async_remote_copy(
+            src_ref=mbuf.at[src],
+            dst_ref=mbuf.at[src],
+            send_sem=msend.at[k],
+            recv_sem=mrecv.at[src],
+            device_id=(src, o),
+            device_id_type=MESH_ID,
+        ).wait_recv()
+    for copy in sends:
+        copy.wait_send()
+    best = mbuf[0]
+    for j in range(1, n_rows):
+        best = jnp.maximum(best, mbuf[j])
+    best_ref[...] = best
+
+
+def exchange_gains(partial_gain, targets):
+    nodes, span = partial_gain.shape
+    n_rows = lax.axis_size("rows")
+    n_outs = lax.axis_size("outs")
+    width = 128
+    return pl.pallas_call(
+        functools.partial(exchange_kernel, targets=targets),
+        out_shape=(
+            jax.ShapeDtypeStruct((nodes, span), jnp.float32),
+            jax.ShapeDtypeStruct((nodes, width), jnp.float32),
+        ),
+        in_specs=[pl.BlockSpec(memory_space=pltpu.VMEM)],
+        out_specs=(pl.BlockSpec(memory_space=pltpu.VMEM), pl.BlockSpec(memory_space=pltpu.VMEM)),
+        scratch_shapes=[
+            pltpu.VMEM((n_outs, nodes, span), jnp.float32),
+            pltpu.VMEM((n_rows, nodes, width), jnp.float32),
+            pltpu.SemaphoreType.DMA((n_outs,)),
+            pltpu.SemaphoreType.DMA((n_outs,)),
+            pltpu.SemaphoreType.DMA((n_rows,)),
+            pltpu.SemaphoreType.DMA((n_rows,)),
+        ],
+        compiler_params=pltpu.CompilerParams(collective_id=0, has_side_effects=True),
+    )(partial_gain)
+
+
 def local(codes, node_of_row, grad, hess, small_side, evicted, parent_hist):
     pairs = small_side.shape[0]
     nodes = 2 * pairs
@@ -100,10 +202,10 @@
     codes_t = lax.all_to_all(
         codes.astype(jnp.int16).T, "rows", 0, 1, tiled=True
     ).astype(jnp.int32)
-    v_t = lax.all_gather(jnp.concatenate([grad.T, hess.T], axis=0), "rows", axis=1, tiled=True)
-    node_all = lax.all_gather(node_of_row.reshape(1, -1), "rows", axis=1, tiled=True)
+    node_row = node_of_row.astype(jnp.bfloat16).reshape(1, -1)
+    v_t = lax.all_gather(jnp.concatenate([grad.T, hess.T, node_row], axis=0), "rows", axis=1, tiled=True)
     span = codes_t.shape[0] * BINS
-    built = build_hist(codes_t, v_t, node_all, nodes).reshape(2, nodes, local_targets, span)
+    built = build_hist(codes_t, v_t, nodes).reshape(2, nodes, local_targets, span)
     small = (small_side == 0)[None, :, None, None]
     pair_view = built.reshape(2, pairs, 2, local_targets, span)
     child = jnp.where(small, pair_view[:, :, 0], pair_view[:, :, 1])
@@ -114,8 +216,8 @@
     second = jnp.where(small, sibling, child)
     node_hist = jnp.stack([first, second], axis=2).reshape(2, nodes, local_targets, span)
     partial_gain = gain_terms(node_hist)
-    split_gain = lax.psum(partial_gain, "outs") / targets
-    best_gain = lax.pmax(jnp.max(split_gain, axis=1), "rows")
+    split_gain, best = exchange_gains(partial_gain, targets)
+    best_gain = best[:, 0]
     return (node_hist, split_gain, best_gain)
 
 

time: 194 us -> 126 us (0.65)
  blocking collectives: 126 us -> 0 us
  waiting for transfers between devices: 12.9 us -> 46.1 us
  Pallas kernels: 22.3 us -> 43.4 us
  local copies, waits for them, and re-layouts: 1.92 us -> 4.56 us
    pmax x1 -> x0, blocking collectives: 69.9 us -> none  [local(): best_gain = lax.pmax(jnp.max(split_gain, axis=1), 'rows')]
    all_gather x1 -> x0, blocking collectives: 33.2 us -> none  [local(): lax.all_gather(node_of_row.reshape(1, -1), 'rows', axis=1, tiled=True)]
    psum x1 -> x0, blocking collectives: 23.1 us -> none  [local(): split_gain = lax.psum(partial_gain, 'outs') / targets]
    pallas_call x0 -> x1, Pallas kernels: none -> 20.6 us  [exchange_gains(): pl.pallas_call(functools.partial(exchange_kernel, targets=targets), out_s...]
    all_gather x1, waiting for transfers between devices: 12.9 us -> 31.3 us  [local(): lax.all_gather(jnp.concatenate([grad.T, hess.T, node_row], axis=0), 'rows...]
    all_to_all x1, waiting for transfers between devices: 0.01 us -> 14.8 us  [local(): lax.all_to_all(codes.astype(jnp.int16).T, 'rows', 0, 1, tiled=True)]
  transfers between devices with their start and end apart: 2 -> 2, of which waited for: 1 -> 2; matrix products, arithmetic and copies ran while one was open for 2% -> 3% of each run, Pallas kernels for 0% -> 0%
where the time goes in v2:
time: 126 us; the launch traced here: 125 us
  waiting for transfers between devices  46.1 us (37%)
  Pallas kernels  43.4 us (34%)
  between operations  14.2 us (11%)
  starting transfers between devices  8.63 us (7%)
  other arithmetic  6.66 us (5%)
  local copies, waits for them, and re-layouts  4.56 us (4%)
    all_gather x1, waiting for transfers between devices, local(): lax.all_gather(jnp.concatenate([grad.T, hess.T, node_row], axis=0), 'rows...  31.3 us
    pallas_call x1, Pallas kernels, build_hist(): pl.pallas_call(functools.partial(hist_kernel, nodes=nodes), out_shape=jax...  22.9 us
    pallas_call x1, Pallas kernels, exchange_gains(): pl.pallas_call(functools.partial(exchange_kernel, targets=targets), out_s...  20.6 us
    all_to_all x1, waiting for transfers between devices, local(): lax.all_to_all(codes.astype(jnp.int16).T, 'rows', 0, 1, tiled=True)  14.8 us
    all_to_all x1, starting transfers between devices, local(): lax.all_to_all(codes.astype(jnp.int16).T, 'rows', 0, 1, tiled=True)  8.59 us
    unnamed x14, local copies, waits for them, and re-layouts  3.23 us
  transfers between devices with their start and end apart: 2, of which 2 were waited for; matrix products, arithmetic and copies ran while one was open for 3% of the time, Pallas kernels for 0%

profile of v2, /device:TPU:1, one launch (start us, length us, event | category | flops | bytes accessed | tf_op | source)
XLA Modules:
  0.0 124.7 jit_solution(4426032365082183597)
XLA Ops:
  7.2 0.0 all-gather.2.cloned.1.call-start
  7.2 0.7 convert_element_type.17
  7.9 1.5 %pad_maximum_fusion.1 = bf16[33,1536]{1,0:T(8,128)(2,1)} fusion(bf16[1,1536]{1,0:T(2,128)(2,1)S(1)} %reshape.49, bf16[16,1536]{1,0:T(8,128)(2,1)} %bitcast.60, bf16[16,1536]{1,0:T(8,128)(2,1)} %bitcast.61), kind=kLoop, calls=%fused_computation.10 | loop fusion | flops 304128 | bytes 202752 | tf_op jit(solution)/shard_map/concatenate | solution.py:206
  9.4 0.0 all-gather.2.cloned.1.call-update
  9.4 1.9 %copy.16 = s32[1536,256]{0,1:T(8,128)S(1)} copy(s32[1536,256]{1,0:T(8,128)} %param.9) | data formatting | bytes 3145728 | tf_op args[0]
  11.3 0.0 copy-start.4
  11.3 0.0 copy-start.5
  11.3 1.0 convert_bitcast_fusion
  12.3 8.6 %all-to-all-start = ((s16[32,8,1536]{2,1,0:T(8,128)(2,1)}), s16[32,8,1536]{2,1,0:T(8,128)(2,1)S(1)}, u32[]{:S(2)}, u32[]{:S(2)}) async-start(s16[32,8,1536]{2,1,0:T(8,128)(2,1)} %convert_bitcast_fusion), calls=%async_computation | async-start | bytes 1572864 | tf_op jit(solution)/shard_map/all_to_all | solution.py:202
  20.9 0.0 copy-done.4
  20.9 0.0 copy-done.5
  21.0 14.8 %all-to-all-done = s16[32,8,1536]{2,1,0:T(8,128)(2,1)S(1)} async-done(((s16[32,8,1536]{2,1,0:T(8,128)(2,1)}), s16[32,8,1536]{2,1,0:T(8,128)(2,1)S(1)}, u32[]{:S(2)}, u32[]{:S(2)}) %all-to-all-start) | async-done | bytes 786464 | tf_op jit(solution)/shard_map/all_to_all | solution.py:202
  35.8 1.4 %convert_element_type.19 = s32[32,8,1536]{2,1,0:T(8,128)} convert(s16[32,8,1536]{2,1,0:T(8,128)(2,1)S(1)} %all-to-all-done) | non-fusion elementwise | flops 393216 | bytes 2359296 | tf_op jit(solution)/shard_map/convert_element_type | solution.py:204
  37.2 31.3 %all-gather.2.cloned.1.call-done.v_ref = bf16[33,49152]{1,0:T(8,128)(2,1)} async-done(((bf16[33,1536]{1,0:T(8,128)(2,1)}), bf16[33,49152]{1,0:T(8,128)(2,1)}) %all-gather.2.cloned.1.call-update) | async-done | bytes 3244048 | tf_op jit(solution)/shard_map/all_gather | solution.py:206
  68.5 0.0 copy-start.3
  68.5 22.9 %shard_map.112 = f32[512,256]{1,0:T(8,128)} custom-call(s32[8,49152]{1,0:T(8,128)} %bitcast.58, bf16[33,49152]{1,0:T(8,128)(2,1)} %all-gather.2.cloned.1.call-done.v_ref), custom_call_target="tpu_custom_call" | custom-call | flops 12884901888 | bytes 5341184 | tf_op jit(solution)/shard_map/pallas_call | solution.py:48
  91.4 0.0 copy-start.1
  91.4 0.0 copy-done.3
  91.4 0.0 copy-start.2
  91.4 1.2 select_bitcast_fusion.1
  92.6 0.0 copy-start
  92.7 0.0 copy-done.1
  92.7 0.6 fusion.1
  93.2 0.0 copy-done.2
  93.3 0.6 fusion.2
  93.8 0.8 bitcast_reduce_fusion.p_ref
  94.7 0.0 copy-done
  94.7 20.6 %shard_map.113 = (f32[16,256]{1,0:T(8,128)}, f32[16,128]{1,0:T(8,128)}) custom-call(f32[16,256]{1,0:T(8,128)} %bitcast_reduce_fusion.p_ref), custom_call_target="tpu_custom_call" | custom-call | tf_op jit(solution)/shard_map/pallas_call | solution.py:177
  115.2 1.3 %slice_reduce_fusion = f32[16]{0:T(128)} fusion(f32[16,128]{1,0:T(8,128)} %get-tuple-element.6), kind=kLoop, calls=%fused_computation.11 | loop fusion | bytes 128 | tf_op jit(solution)/shard_map/slice | solution.py:220
  116.5 1.3 %copy.23 = f32[16,256]{1,0:T(8,128)} copy(f32[16,256]{1,0:T(8,128)} %get-tuple-element.15) | data formatting | bytes 32768
  (3 shorter events, 0.1 us)
Async XLA Ops:
  7.2 61.3 %all-gather.2.cloned.1.call-start = ((), (), s32[]{:S(2)}) async-start(), calls=%async_computation.1 | async-start | bytes 4055040 | tf_op jit(solution)/shard_map/all_gather | solution.py:206
  11.3 9.6 %copy-start.4 = (s32[8]{0:T(128)S(1)}, s32[8]{0:T(128)}, u32[]{:S(2)}) copy-start(s32[8]{0:T(128)} %param.14) | copy-start | bytes 100
  11.3 9.6 %copy-start.5 = (s32[8]{0:T(128)S(1)}, s32[8]{0:T(128)}, u32[]{:S(2)}) copy-start(s32[8]{0:T(128)} %param.13) | copy-start | bytes 100
  12.3 23.5 %all-to-all-start = ((s16[32,8,1536]{2,1,0:T(8,128)(2,1)}), s16[32,8,1536]{2,1,0:T(8,128)(2,1)S(1)}, u32[]{:S(2)}, u32[]{:S(2)}) async-start(s16[32,8,1536]{2,1,0:T(8,128)(2,1)} %convert_bitcast_fusion), calls=%async_computation | async-start | bytes 1572864 | tf_op jit(solution)/shard_map/all_to_all | solution.py:202
  68.5 22.9 %copy-start.3 = (f32[2,8,16,256]{3,2,1,0:T(8,128)S(1)}, f32[2,8,16,256]{3,2,1,0:T(8,128)}, u32[]{:S(2)}) copy-start(f32[2,8,16,256]{3,2,1,0:T(8,128)} %param.15) | copy-start | bytes 786436
  91.4 1.3 %copy-start.1 = (f32[256,256]{1,0:T(8,128)S(1)}, f32[256,256]{1,0:T(8,128)}, u32[]{:S(2)}) copy-start(f32[256,256]{1,0:T(8,128)} %constant.5.clone) | copy-start | bytes 786436
  91.4 1.9 %copy-start.2 = (f32[256,256]{1,0:T(8,128)S(1)}, f32[256,256]{1,0:T(8,128)}, u32[]{:S(2)}) copy-start(f32[256,256]{1,0:T(8,128)} %constant.14.clone) | copy-start | bytes 786436
  92.6 2.0 %copy-start = (f32[2,8,2,16,256]{4,3,2,1,0:T(8,128)}, f32[2,8,2,16,256]{4,3,2,1,0:T(8,128)S(1)}, u32[]{:S(2)}) copy-start(f32[2,8,2,16,256]{4,3,2,1,0:T(8,128)S(1)} %pad_maximum_fusion) | copy-start | bytes 1572868
Sparse Core Ops, SparseCore 0:
  11.2 57.2 all-gather.1

commit v3 on v2

--- a/solution.py
+++ b/solution.py
@@ -9,57 +9,6 @@
 from jax.sharding import PartitionSpec as P
 
 BINS = 32
-ROW_TILE = 2048
-
-
-def hist_kernel(codes_ref, v_ref, out_ref, *, nodes):
-    @pl.when(pl.program_id(0) == 0)
-    def _():
-        out_ref[...] = jnp.zeros_like(out_ref)
-
-    feats, rows = codes_ref.shape
-    one = jnp.ones((), jnp.bfloat16)
-    zero = jnp.zeros((), jnp.bfloat16)
-    bins = lax.broadcasted_iota(jnp.int32, (BINS, rows), 0)
-    onehot = jnp.concatenate(
-        [jnp.where(codes_ref[f : f + 1, :] == bins, one, zero) for f in range(feats)], axis=0
-    )
-    v = v_ref[...]
-    tl = v.shape[0] // 2
-    node = v[2 * tl : 2 * tl + 1]
-    blocks = []
-    for c in range(2):
-        vc = v[c * tl : (c + 1) * tl]
-        for n in range(nodes):
-            blocks.append(jnp.where(node == jnp.asarray(n, jnp.bfloat16), vc, zero))
-    vals = jnp.concatenate(blocks, axis=0)
-    out_ref[...] += lax.dot_general(
-        vals, onehot, (((1,), (1,)), ((), ())), preferred_element_type=jnp.float32
-    )
-
-
-def build_hist(codes_t, v_t, nodes):
-    feats, total = codes_t.shape
-    width = v_t.shape[0]
-    tile = min(ROW_TILE, total)
-    steps = total // tile
-    out_rows = (width - 1) * nodes
-    cols = feats * BINS
-    return pl.pallas_call(
-        functools.partial(hist_kernel, nodes=nodes),
-        out_shape=jax.ShapeDtypeStruct((out_rows, cols), jnp.float32),
-        grid=(steps,),
-        in_specs=[
-            pl.BlockSpec((feats, tile), lambda i: (0, i)),
-            pl.BlockSpec((width, tile), lambda i: (0, i)),
-        ],
-        out_specs=pl.BlockSpec((out_rows, cols), lambda i: (0, 0)),
-        cost_estimate=pl.CostEstimate(
-            flops=2 * out_rows * cols * total,
-            bytes_accessed=total * (feats * 4 + width * 2) + out_rows * cols * 4,
-            transcendentals=0,
-        ),
-    )(codes_t, v_t)
 
 
 def prefix_matrices(span):
@@ -194,18 +143,127 @@
     )(partial_gain)
 
 
+def block_hist(acc_ref, v, s, nodes):
+    tl = v.shape[0] // 2
+    half = s.shape[1]
+    feats = s.shape[0] // 2
+    one = jnp.ones((), jnp.bfloat16)
+    zero = jnp.zeros((), jnp.bfloat16)
+    bins = lax.broadcasted_iota(jnp.int32, (BINS, half), 0)
+    for h in range(2):
+        vh = v[:, h * half : (h + 1) * half]
+        node = s[h : h + 1] >> 5
+        onehot = jnp.concatenate(
+            [jnp.where((s[2 * f + h : 2 * f + h + 1] & (BINS - 1)) == bins, one, zero) for f in range(feats)],
+            axis=0,
+        )
+        blocks = []
+        for c in range(2):
+            vc = vh[c * tl : (c + 1) * tl]
+            for n in range(nodes):
+                blocks.append(jnp.where(node == n, vc, zero))
+        vals = jnp.concatenate(blocks, axis=0)
+        acc_ref[...] += lax.dot_general(
+            vals, onehot, (((1,), (1,)), ((), ())), preferred_element_type=jnp.float32
+        )
+
+
+def gather_hist_kernel(seg_ref, v_ref, acc_ref, vbuf, sbuf, vsend, vrecv, ssend, srecv, *, nodes):
+    n_rows = lax.axis_size("rows")
+    r = lax.axis_index("rows")
+    o = lax.axis_index("outs")
+    barrier = pltpu.get_barrier_semaphore()
+
+    def greet(k, carry):
+        pl.semaphore_signal(barrier, 1, device_id=((r + k) % n_rows, o), device_id_type=MESH_ID)
+        return carry
+
+    lax.fori_loop(1, n_rows, greet, 0)
+    pl.semaphore_wait(barrier, n_rows - 1)
+
+    def v_copy(k, peer, slot):
+        return pltpu.make_async_remote_copy(
+            src_ref=v_ref, dst_ref=vbuf.at[slot], send_sem=vsend.at[k], recv_sem=vrecv.at[slot],
+            device_id=(peer, o), device_id_type=MESH_ID,
+        )
+
+    def s_copy(k, peer, slot):
+        return pltpu.make_async_remote_copy(
+            src_ref=seg_ref.at[peer], dst_ref=sbuf.at[slot], send_sem=ssend.at[k], recv_sem=srecv.at[slot],
+            device_id=(peer, o), device_id_type=MESH_ID,
+        )
+
+    def send(k, carry):
+        peer = (r + k) % n_rows
+        v_copy(k, peer, r).start()
+        s_copy(k, peer, r).start()
+        return carry
+
+    lax.fori_loop(1, n_rows, send, 0)
+    acc_ref[...] = jnp.zeros_like(acc_ref)
+    block_hist(acc_ref, v_ref[...], seg_ref[r].astype(jnp.int32), nodes)
+
+    def take(k, carry):
+        src = (r + n_rows - k) % n_rows
+        v_copy(k, src, src).wait_recv()
+        s_copy(k, src, src).wait_recv()
+        block_hist(acc_ref, vbuf[src], sbuf[src].astype(jnp.int32), nodes)
+        return carry
+
+    lax.fori_loop(1, n_rows, take, 0)
+
+    def drain(k, carry):
+        peer = (r + k) % n_rows
+        v_copy(k, peer, r).wait_send()
+        s_copy(k, peer, r).wait_send()
+        return carry
+
+    lax.fori_loop(1, n_rows, drain, 0)
+
+
+def gather_hist(seg_p, v_loc, nodes):
+    n_rows, width, half = seg_p.shape
+    vw, rows = v_loc.shape
+    feats = width // 2
+    out_rows = vw * nodes
+    cols = feats * BINS
+    total = n_rows * rows
+    return pl.pallas_call(
+        functools.partial(gather_hist_kernel, nodes=nodes),
+        out_shape=jax.ShapeDtypeStruct((out_rows, cols), jnp.float32),
+        in_specs=[pl.BlockSpec(memory_space=pltpu.VMEM)] * 2,
+        out_specs=pl.BlockSpec(memory_space=pltpu.VMEM),
+        scratch_shapes=[
+            pltpu.VMEM((n_rows, vw, rows), v_loc.dtype),
+            pltpu.VMEM((n_rows, width, half), seg_p.dtype),
+            pltpu.SemaphoreType.DMA((n_rows,)),
+            pltpu.SemaphoreType.DMA((n_rows,)),
+            pltpu.SemaphoreType.DMA((n_rows,)),
+            pltpu.SemaphoreType.DMA((n_rows,)),
+        ],
+        compiler_params=pltpu.CompilerParams(collective_id=1, has_side_effects=True),
+        cost_estimate=pl.CostEstimate(
+            flops=2 * out_rows * cols * total,
+            bytes_accessed=total * (vw * 2 + feats * 2) + out_rows * cols * 4,
+            transcendentals=0,
+        ),
+    )(seg_p, v_loc)
+
+
 def local(codes, node_of_row, grad, hess, small_side, evicted, parent_hist):
     pairs = small_side.shape[0]
     nodes = 2 * pairs
     local_targets = grad.shape[1]
     targets = local_targets * lax.axis_size("outs")
-    codes_t = lax.all_to_all(
-        codes.astype(jnp.int16).T, "rows", 0, 1, tiled=True
-    ).astype(jnp.int32)
-    node_row = node_of_row.astype(jnp.bfloat16).reshape(1, -1)
-    v_t = lax.all_gather(jnp.concatenate([grad.T, hess.T, node_row], axis=0), "rows", axis=1, tiled=True)
-    span = codes_t.shape[0] * BINS
-    built = build_hist(codes_t, v_t, nodes).reshape(2, nodes, local_targets, span)
+    n_rows = lax.axis_size("rows")
+    count, features = codes.shape
+    feats = features // n_rows
+    half = count // 2
+    seg = (node_of_row[:, None] * BINS + codes).astype(jnp.int16)
+    seg_p = jnp.transpose(seg.reshape(2, half, n_rows, feats), (2, 3, 0, 1)).reshape(n_rows, 2 * feats, half)
+    v_loc = jnp.concatenate([grad.T, hess.T], axis=0)
+    span = feats * BINS
+    built = gather_hist(seg_p, v_loc, nodes).reshape(2, nodes, local_targets, span)
     small = (small_side == 0)[None, :, None, None]
     pair_view = built.reshape(2, pairs, 2, local_targets, span)
     child = jnp.where(small, pair_view[:, :, 0], pair_view[:, :, 1])

time: 126 us -> 109 us (0.87)
  Pallas kernels: 43.4 us -> 96.5 us
  waiting for transfers between devices: 46.1 us -> 0 us
  between operations: 14.2 us -> 0.76 us
  starting transfers between devices: 8.63 us -> 0 us
    pallas_call x1, Pallas kernels: 22.9 us -> 74.5 us  [gather_hist(): pl.pallas_call(functools.partial(gather_hist_kernel, nodes=nodes), out_sh...]
    all_gather x1 -> x0, waiting for transfers between devices: 31.3 us -> none  [local(): lax.all_gather(jnp.concatenate([grad.T, hess.T, node_row], axis=0), 'rows...]
    all_to_all x1 -> x0, waiting for transfers between devices: 14.8 us -> none  [local(): lax.all_to_all(codes.astype(jnp.int16).T, 'rows', 0, 1, tiled=True)]
    all_to_all x1 -> x0, starting transfers between devices: 8.59 us -> none  [local(): lax.all_to_all(codes.astype(jnp.int16).T, 'rows', 0, 1, tiled=True)]
    unnamed x14 -> x13, local copies, waits for them, and re-layouts: 3.23 us -> 1.36 us
    reshape x1 -> x2, local copies, waits for them, and re-layouts: 0.01 us -> 1.43 us  [the longest x1 1.21 us: local(): jnp.transpose(seg.reshape(2, half, n_rows, feats), (2, 3, 0, 1))]
    pallas_call x1, Pallas kernels: 20.6 us -> 21.9 us  [exchange_gains(): pl.pallas_call(functools.partial(exchange_kernel, targets=targets), out_s...]
  transfers between devices with their start and end apart: 2 -> 0, of which waited for: 2 -> 0; matrix products, arithmetic and copies ran while one was open for 3% -> 0% of each run, Pallas kernels for 0% -> 0%
where the time goes in v3:
time: 109 us
  Pallas kernels  96.5 us (89%)
  other arithmetic  5.76 us (5%)
  local copies, waits for them, and re-layouts  4.78 us (4%)
  matrix products  1.16 us (1%)
    pallas_call x1, Pallas kernels, gather_hist(): pl.pallas_call(functools.partial(gather_hist_kernel, nodes=nodes), out_sh...  74.5 us
    pallas_call x1, Pallas kernels, exchange_gains(): pl.pallas_call(functools.partial(exchange_kernel, targets=targets), out_s...  21.9 us

profile of v3, /device:TPU:1, one launch (start us, length us, event | category | flops | bytes accessed | tf_op | source)
XLA Modules:
  0.0 108.9 jit_solution(5218648235970142004)
XLA Ops:
  0.6 0.7 broadcast_compare_fusion
  1.3 0.7 broadcast_multiply_fusion
  2.0 1.7 %add_convert_fusion = s16[1536,256]{1,0:T(8,128)(2,1)S(1)} fusion(s32[1536,256]{1,0:T(8,128)} %param.9, s32[1536]{0:T(1024)S(1)} %broadcast_multiply_fusion), kind=kLoop, calls=%fused_computation | loop fusion | flops 786432 | bytes 2365440 | tf_op jit(solution)/shard_map/convert_element_type | solution.py:262
  3.7 0.7 copy.16
  4.4 0.0 copy-start.4
  4.4 0.0 copy-start.5
  4.4 0.2 reshape.49
  4.6 1.2 %reshape.50.seg_ref = s16[32,16,768]{2,1,0:T(8,128)(2,1)} reshape(s16[32,8,2,768]{3,2,1,0:T(2,128)(2,1)S(1)} %bitcast.52) | data formatting | bytes 1572864 | tf_op jit(solution)/shard_map/reshape | solution.py:263
  5.8 0.0 copy-done.4
  5.8 0.0 copy-done.5
  5.8 0.6 pad_maximum_fusion.1.v_ref
  6.5 0.0 copy-start.3
  6.5 74.5 %shard_map.112 = f32[512,256]{1,0:T(8,128)} custom-call(s16[32,16,768]{2,1,0:T(8,128)(2,1)} %reshape.50.seg_ref, bf16[32,1536]{1,0:T(8,128)(2,1)} %pad_maximum_fusion.1.v_ref), custom_call_target="tpu_custom_call" | custom-call | flops 12884901888 | bytes 4456448 | tf_op jit(solution)/shard_map/pallas_call | solution.py:231
  81.0 0.0 copy-start.1
  81.0 0.0 copy-done.3
  81.0 0.0 copy-start.2
  81.0 1.2 %select_bitcast_fusion.1 = (f32[2,8,1,16,256]{4,3,2,1,0:T(8,128)S(1)}, f32[2,8,1,16,256]{4,3,2,1,0:T(8,128)S(1)}) fusion(pred[8]{0:T(512)(128)(4,1)S(1)} %get-tuple-element.10, f32[2,8,16,256]{3,2,1,0:T(8,128)S(1)} %copy-done.3, f32[2,8,2,16,256]{4,3,2,1,0:T(8,128)} %bitcast.55, pred[8]{0:T(512)(128)(4,1)S(1)} %get-tuple-element.9), kind=kLoop, calls=%fused_computation.7 | loop fusion | flops 393216 | bytes 1310736 | tf_op jit(solution)/shard_map/stack | solution.py:275
  82.3 0.0 copy-start
  82.3 0.0 copy-done.1
  82.3 0.6 fusion.1
  82.9 0.0 copy-done.2
  82.9 0.6 fusion.2
  83.5 0.8 bitcast_reduce_fusion.p_ref
  84.3 0.0 copy-done
  84.3 21.9 %shard_map.113 = (f32[16,256]{1,0:T(8,128)}, f32[16,128]{1,0:T(8,128)}) custom-call(f32[16,256]{1,0:T(8,128)} %bitcast_reduce_fusion.p_ref), custom_call_target="tpu_custom_call" | custom-call | tf_op jit(solution)/shard_map/pallas_call | solution.py:126
  106.3 1.3 %slice_reduce_fusion = f32[16]{0:T(128)} fusion(f32[16,128]{1,0:T(8,128)} %get-tuple-element.6), kind=kLoop, calls=%fused_computation.11 | loop fusion | bytes 128 | tf_op jit(solution)/shard_map/slice | solution.py:278
  107.6 1.3 %copy.23 = f32[16,256]{1,0:T(8,128)} copy(f32[16,256]{1,0:T(8,128)} %get-tuple-element.15) | data formatting | bytes 32768
  (1 shorter events, 0.0 us)
Async XLA Ops:
  4.4 1.5 %copy-start.4 = (bf16[1536,16]{0,1:T(8,128)(2,1)S(1)}, bf16[1536,16]{0,1:T(8,128)(2,1)}, u32[]{:S(2)}) copy-start(bf16[1536,16]{0,1:T(8,128)(2,1)} %param.12) | copy-start | bytes 147460
  4.4 1.4 %copy-start.5 = (bf16[1536,16]{0,1:T(8,128)(2,1)S(1)}, bf16[1536,16]{0,1:T(8,128)(2,1)}, u32[]{:S(2)}) copy-start(bf16[1536,16]{0,1:T(8,128)(2,1)} %param.11) | copy-start | bytes 147460
  6.5 74.5 %copy-start.3 = (f32[2,8,16,256]{3,2,1,0:T(8,128)S(1)}, f32[2,8,16,256]{3,2,1,0:T(8,128)}, u32[]{:S(2)}) copy-start(f32[2,8,16,256]{3,2,1,0:T(8,128)} %param.15) | copy-start | bytes 786436
  81.0 1.3 %copy-start.1 = (f32[256,256]{1,0:T(8,128)S(1)}, f32[256,256]{1,0:T(8,128)}, u32[]{:S(2)}) copy-start(f32[256,256]{1,0:T(8,128)} %constant.6.clone) | copy-start | bytes 786436
  81.0 1.9 %copy-start.2 = (f32[256,256]{1,0:T(8,128)S(1)}, f32[256,256]{1,0:T(8,128)}, u32[]{:S(2)}) copy-start(f32[256,256]{1,0:T(8,128)} %constant.16.clone) | copy-start | bytes 786436
  82.3 2.0 %copy-start = (f32[2,8,2,16,256]{4,3,2,1,0:T(8,128)}, f32[2,8,2,16,256]{4,3,2,1,0:T(8,128)S(1)}, u32[]{:S(2)}) copy-start(f32[2,8,2,16,256]{4,3,2,1,0:T(8,128)S(1)} %pad_maximum_fusion) | copy-start | bytes 1572868

commit v4 on v3

--- a/solution.py
+++ b/solution.py
@@ -168,10 +168,14 @@
         )
 
 
-def gather_hist_kernel(seg_ref, v_ref, acc_ref, vbuf, sbuf, vsend, vrecv, ssend, srecv, *, nodes):
+def gather_hist_kernel(seg_ref, v_ref, acc_ref, vbuf, sbuf, vsend, fsend, vrecv, ssend, srecv, *, nodes):
     n_rows = lax.axis_size("rows")
+    chips = n_rows // 2
     r = lax.axis_index("rows")
     o = lax.axis_index("outs")
+    core = r % 2
+    chip = r // 2
+    partner = chip * 2 + 1 - core
     barrier = pltpu.get_barrier_semaphore()
 
     def greet(k, carry):
@@ -180,6 +184,12 @@
 
     lax.fori_loop(1, n_rows, greet, 0)
     pl.semaphore_wait(barrier, n_rows - 1)
+
+    def s_copy(k, peer, slot):
+        return pltpu.make_async_remote_copy(
+            src_ref=seg_ref.at[peer], dst_ref=sbuf.at[slot], send_sem=ssend.at[k], recv_sem=srecv.at[slot],
+            device_id=(peer, o), device_id_type=MESH_ID,
+        )
 
     def v_copy(k, peer, slot):
         return pltpu.make_async_remote_copy(
@@ -187,38 +197,69 @@
             device_id=(peer, o), device_id_type=MESH_ID,
         )
 
-    def s_copy(k, peer, slot):
+    def f_copy(k, slot):
         return pltpu.make_async_remote_copy(
-            src_ref=seg_ref.at[peer], dst_ref=sbuf.at[slot], send_sem=ssend.at[k], recv_sem=srecv.at[slot],
-            device_id=(peer, o), device_id_type=MESH_ID,
-        )
+            src_ref=vbuf.at[slot], dst_ref=vbuf.at[slot], send_sem=fsend.at[k], recv_sem=vrecv.at[slot],
+            device_id=(partner, o), device_id_type=MESH_ID,
+        )
+
+    own = pltpu.make_async_remote_copy(
+        src_ref=v_ref, dst_ref=vbuf.at[r], send_sem=fsend.at[0], recv_sem=vrecv.at[r],
+        device_id=(partner, o), device_id_type=MESH_ID,
+    )
+    own.start()
 
     def send(k, carry):
-        peer = (r + k) % n_rows
-        v_copy(k, peer, r).start()
-        s_copy(k, peer, r).start()
-        return carry
-
-    lax.fori_loop(1, n_rows, send, 0)
+        v_copy(k, ((chip + k) % chips) * 2 + core, r).start()
+        return carry
+
+    lax.fori_loop(1, chips, send, 0)
+
+    def send_seg(k, carry):
+        s_copy(k, (r + k) % n_rows, r).start()
+        return carry
+
+    lax.fori_loop(1, n_rows, send_seg, 0)
     acc_ref[...] = jnp.zeros_like(acc_ref)
     block_hist(acc_ref, v_ref[...], seg_ref[r].astype(jnp.int32), nodes)
 
-    def take(k, carry):
-        src = (r + n_rows - k) % n_rows
+    def take_direct(k, carry):
+        src = ((chip + chips - k) % chips) * 2 + core
         v_copy(k, src, src).wait_recv()
+        f_copy(k, src).start()
         s_copy(k, src, src).wait_recv()
         block_hist(acc_ref, vbuf[src], sbuf[src].astype(jnp.int32), nodes)
         return carry
 
-    lax.fori_loop(1, n_rows, take, 0)
+    lax.fori_loop(1, chips, take_direct, 0)
+
+    def take_forwarded(k, carry):
+        src = ((chip + chips - k) % chips) * 2 + 1 - core
+        f_copy(k, src).wait_recv()
+        s_copy(k, src, src).wait_recv()
+        block_hist(acc_ref, vbuf[src], sbuf[src].astype(jnp.int32), nodes)
+        return carry
+
+    lax.fori_loop(0, chips, take_forwarded, 0)
 
     def drain(k, carry):
-        peer = (r + k) % n_rows
-        v_copy(k, peer, r).wait_send()
-        s_copy(k, peer, r).wait_send()
+        s_copy(k, (r + k) % n_rows, r).wait_send()
         return carry
 
     lax.fori_loop(1, n_rows, drain, 0)
+
+    def drain_v(k, carry):
+        v_copy(k, ((chip + k) % chips) * 2 + core, r).wait_send()
+        return carry
+
+    lax.fori_loop(1, chips, drain_v, 0)
+    own.wait_send()
+
+    def drain_f(k, carry):
+        f_copy(k, ((chip + chips - k) % chips) * 2 + core).wait_send()
+        return carry
+
+    lax.fori_loop(1, chips, drain_f, 0)
 
 
 def gather_hist(seg_p, v_loc, nodes):
@@ -236,7 +277,8 @@
         scratch_shapes=[
             pltpu.VMEM((n_rows, vw, rows), v_loc.dtype),
             pltpu.VMEM((n_rows, width, half), seg_p.dtype),
-            pltpu.SemaphoreType.DMA((n_rows,)),
+            pltpu.SemaphoreType.DMA((n_rows // 2,)),
+            pltpu.SemaphoreType.DMA((n_rows // 2,)),
             pltpu.SemaphoreType.DMA((n_rows,)),
             pltpu.SemaphoreType.DMA((n_rows,)),
             pltpu.SemaphoreType.DMA((n_rows,)),

time: 109 us -> 91.3 us (0.84)
  Pallas kernels: 96.5 us -> 78.4 us
    pallas_call x1, Pallas kernels: 74.5 us -> 55.8 us  [gather_hist(): pl.pallas_call(functools.partial(gather_hist_kernel, nodes=nodes), out_sh...]
where the time goes in v4:
time: 91.3 us; the launch traced here: 90.9 us
  Pallas kernels  78.4 us (86%)
  other arithmetic  5.76 us (6%)
  local copies, waits for them, and re-layouts  4.78 us (5%)
  matrix products  1.16 us (1%)
    pallas_call x1, Pallas kernels, gather_hist(): pl.pallas_call(functools.partial(gather_hist_kernel, nodes=nodes), out_sh...  55.8 us
    pallas_call x1, Pallas kernels, exchange_gains(): pl.pallas_call(functools.partial(exchange_kernel, targets=targets), out_s...  22.7 us

profile of v4, /device:TPU:1, one launch (start us, length us, event | category | flops | bytes accessed | tf_op | source)
XLA Modules:
  0.0 90.9 jit_solution(14820623473227131415)
XLA Ops:
  0.6 0.7 broadcast_compare_fusion
  1.3 0.7 broadcast_multiply_fusion
  2.0 1.7 %add_convert_fusion = s16[1536,256]{1,0:T(8,128)(2,1)S(1)} fusion(s32[1536,256]{1,0:T(8,128)} %param.9, s32[1536]{0:T(1024)S(1)} %broadcast_multiply_fusion), kind=kLoop, calls=%fused_computation | loop fusion | flops 786432 | bytes 2365440 | tf_op jit(solution)/shard_map/convert_element_type | solution.py:304
  3.7 0.7 copy.16
  4.4 0.0 copy-start.4
  4.4 0.0 copy-start.5
  4.4 0.2 reshape.49
  4.6 1.2 %reshape.50.seg_ref = s16[32,16,768]{2,1,0:T(8,128)(2,1)} reshape(s16[32,8,2,768]{3,2,1,0:T(2,128)(2,1)S(1)} %bitcast.52) | data formatting | bytes 1572864 | tf_op jit(solution)/shard_map/reshape | solution.py:305
  5.8 0.0 copy-done.4
  5.8 0.0 copy-done.5
  5.8 0.6 pad_maximum_fusion.1.v_ref
  6.5 0.0 copy-start.3
  6.5 55.8 %shard_map.112 = f32[512,256]{1,0:T(8,128)} custom-call(s16[32,16,768]{2,1,0:T(8,128)(2,1)} %reshape.50.seg_ref, bf16[32,1536]{1,0:T(8,128)(2,1)} %pad_maximum_fusion.1.v_ref), custom_call_target="tpu_custom_call" | custom-call | flops 12884901888 | bytes 4456448 | tf_op jit(solution)/shard_map/pallas_call | solution.py:272
  62.3 0.0 copy-start.1
  62.3 0.0 copy-done.3
  62.3 0.0 copy-start.2
  62.3 1.2 %select_bitcast_fusion.1 = (f32[2,8,1,16,256]{4,3,2,1,0:T(8,128)S(1)}, f32[2,8,1,16,256]{4,3,2,1,0:T(8,128)S(1)}) fusion(pred[8]{0:T(512)(128)(4,1)S(1)} %get-tuple-element.10, f32[2,8,16,256]{3,2,1,0:T(8,128)S(1)} %copy-done.3, f32[2,8,2,16,256]{4,3,2,1,0:T(8,128)} %bitcast.55, pred[8]{0:T(512)(128)(4,1)S(1)} %get-tuple-element.9), kind=kLoop, calls=%fused_computation.7 | loop fusion | flops 393216 | bytes 1310736 | tf_op jit(solution)/shard_map/stack | solution.py:317
  63.6 0.0 copy-start
  63.6 0.0 copy-done.1
  63.6 0.6 fusion.1
  64.2 0.0 copy-done.2
  64.2 0.6 fusion.2
  64.8 0.8 bitcast_reduce_fusion.p_ref
  65.6 0.0 copy-done
  65.6 22.7 %shard_map.113 = (f32[16,256]{1,0:T(8,128)}, f32[16,128]{1,0:T(8,128)}) custom-call(f32[16,256]{1,0:T(8,128)} %bitcast_reduce_fusion.p_ref), custom_call_target="tpu_custom_call" | custom-call | tf_op jit(solution)/shard_map/pallas_call | solution.py:126
  88.3 1.3 %slice_reduce_fusion = f32[16]{0:T(128)} fusion(f32[16,128]{1,0:T(8,128)} %get-tuple-element.6), kind=kLoop, calls=%fused_computation.11 | loop fusion | bytes 128 | tf_op jit(solution)/shard_map/slice | solution.py:320
  89.6 1.3 %copy.23 = f32[16,256]{1,0:T(8,128)} copy(f32[16,256]{1,0:T(8,128)} %get-tuple-element.15) | data formatting | bytes 32768
  (1 shorter events, 0.0 us)
Async XLA Ops:
  4.4 1.5 %copy-start.4 = (bf16[1536,16]{0,1:T(8,128)(2,1)S(1)}, bf16[1536,16]{0,1:T(8,128)(2,1)}, u32[]{:S(2)}) copy-start(bf16[1536,16]{0,1:T(8,128)(2,1)} %param.12) | copy-start | bytes 147460
  4.4 1.4 %copy-start.5 = (bf16[1536,16]{0,1:T(8,128)(2,1)S(1)}, bf16[1536,16]{0,1:T(8,128)(2,1)}, u32[]{:S(2)}) copy-start(bf16[1536,16]{0,1:T(8,128)(2,1)} %param.11) | copy-start | bytes 147460
  6.5 55.8 %copy-start.3 = (f32[2,8,16,256]{3,2,1,0:T(8,128)S(1)}, f32[2,8,16,256]{3,2,1,0:T(8,128)}, u32[]{:S(2)}) copy-start(f32[2,8,16,256]{3,2,1,0:T(8,128)} %param.15) | copy-start | bytes 786436
  62.3 1.3 %copy-start.1 = (f32[256,256]{1,0:T(8,128)S(1)}, f32[256,256]{1,0:T(8,128)}, u32[]{:S(2)}) copy-start(f32[256,256]{1,0:T(8,128)} %constant.6.clone) | copy-start | bytes 786436
  62.3 1.9 %copy-start.2 = (f32[256,256]{1,0:T(8,128)S(1)}, f32[256,256]{1,0:T(8,128)}, u32[]{:S(2)}) copy-start(f32[256,256]{1,0:T(8,128)} %constant.16.clone) | copy-start | bytes 786436
  63.6 2.0 %copy-start = (f32[2,8,2,16,256]{4,3,2,1,0:T(8,128)}, f32[2,8,2,16,256]{4,3,2,1,0:T(8,128)S(1)}, u32[]{:S(2)}) copy-start(f32[2,8,2,16,256]{4,3,2,1,0:T(8,128)S(1)} %pad_maximum_fusion) | copy-start | bytes 1572868

commit v5 on v4

--- a/solution.py
+++ b/solution.py
@@ -43,6 +43,26 @@
 MESH_ID = pl.DeviceIdType.MESH
 
 
+def row_stages(r, n_rows):
+    chips = n_rows // 2
+    nx = 4 if chips % 4 == 0 else chips
+    ny = chips // nx
+    chip = r // 2
+    core = r % 2
+    y = chip // nx
+    x = chip % nx
+    stages = [
+        [chip * 2 + 1 - core],
+        [(y * nx + (x + k) % nx) * 2 + core for k in range(1, nx)],
+        [(((y + k) % ny) * nx + x) * 2 + core for k in range(1, ny)],
+    ]
+    return [stage for stage in stages if stage]
+
+
+def row_peers(r, n_rows):
+    return [peer for stage in row_stages(r, n_rows) for peer in stage]
+
+
 def exchange_kernel(p_ref, split_ref, best_ref, gbuf, mbuf, gsend, grecv, msend, mrecv, *, targets):
     n_rows = lax.axis_size("rows")
     n_outs = lax.axis_size("outs")
@@ -51,9 +71,9 @@
     barrier = pltpu.get_barrier_semaphore()
     for k in range(1, n_outs):
         pl.semaphore_signal(barrier, 1, device_id=(r, (o + k) % n_outs), device_id_type=MESH_ID)
-    for k in range(1, n_rows):
-        pl.semaphore_signal(barrier, 1, device_id=((r + k) % n_rows, o), device_id_type=MESH_ID)
-    pl.semaphore_wait(barrier, n_outs - 1 + n_rows - 1)
+    for peer in row_peers(r, n_rows):
+        pl.semaphore_signal(barrier, 1, device_id=(peer, o), device_id_type=MESH_ID)
+    pl.semaphore_wait(barrier, n_outs - 1 + len(row_peers(r, n_rows)))
 
     sends = []
     for k in range(1, n_outs):
@@ -86,35 +106,29 @@
     split = acc / targets
     split_ref[...] = split
     width = mbuf.shape[2]
-    mbuf[r] = jnp.broadcast_to(jnp.max(split, axis=1, keepdims=True), (split.shape[0], width))
-
-    sends = []
-    for k in range(1, n_rows):
-        copy = pltpu.make_async_remote_copy(
-            src_ref=mbuf.at[r],
-            dst_ref=mbuf.at[r],
-            send_sem=msend.at[k],
-            recv_sem=mrecv.at[r],
-            device_id=((r + k) % n_rows, o),
-            device_id_type=MESH_ID,
-        )
-        copy.start()
-        sends.append(copy)
-    for k in range(1, n_rows):
-        src = (r + n_rows - k) % n_rows
-        pltpu.make_async_remote_copy(
-            src_ref=mbuf.at[src],
-            dst_ref=mbuf.at[src],
-            send_sem=msend.at[k],
-            recv_sem=mrecv.at[src],
-            device_id=(src, o),
-            device_id_type=MESH_ID,
-        ).wait_recv()
-    for copy in sends:
-        copy.wait_send()
-    best = mbuf[0]
-    for j in range(1, n_rows):
-        best = jnp.maximum(best, mbuf[j])
+    best = jnp.broadcast_to(jnp.max(split, axis=1, keepdims=True), (split.shape[0], width))
+    base = 0
+    for peers in row_stages(r, n_rows):
+        mbuf[base] = best
+        sends = []
+        for j, peer in enumerate(peers):
+            copy = pltpu.make_async_remote_copy(
+                src_ref=mbuf.at[base],
+                dst_ref=mbuf.at[base + 1 + j],
+                send_sem=msend.at[base + 1 + j],
+                recv_sem=mrecv.at[base + 1 + j],
+                device_id=(peer, o),
+                device_id_type=MESH_ID,
+            )
+            copy.start()
+            sends.append(copy)
+        for copy in sends:
+            copy.wait_recv()
+        for copy in sends:
+            copy.wait_send()
+        for j in range(len(peers)):
+            best = jnp.maximum(best, mbuf[base + 1 + j])
+        base += len(peers) + 1
     best_ref[...] = best
 
 

time: 91.3 us -> 89.9 us (0.985)
  Pallas kernels: 78.4 us -> 77 us
    pallas_call x1, Pallas kernels: 22.7 us -> 21.2 us  [exchange_gains(): pl.pallas_call(functools.partial(exchange_kernel, targets=targets), out_s...]
where the time goes in v5:
time: 89.9 us; the launch traced here: 89.5 us
  Pallas kernels  77 us (86%)
  other arithmetic  5.76 us (6%)
  local copies, waits for them, and re-layouts  4.78 us (5%)
  matrix products  1.16 us (1%)
    pallas_call x1, Pallas kernels, gather_hist(): pl.pallas_call(functools.partial(gather_hist_kernel, nodes=nodes), out_sh...  55.8 us
    pallas_call x1, Pallas kernels, exchange_gains(): pl.pallas_call(functools.partial(exchange_kernel, targets=targets), out_s...  21.2 us

profile of v5, /device:TPU:1, one launch (start us, length us, event | category | flops | bytes accessed | tf_op | source)
XLA Modules:
  0.0 89.5 jit_solution(9858047410525548569)
XLA Ops:
  0.6 0.7 broadcast_compare_fusion
  1.3 0.7 broadcast_multiply_fusion
  2.0 1.7 %add_convert_fusion = s16[1536,256]{1,0:T(8,128)(2,1)S(1)} fusion(s32[1536,256]{1,0:T(8,128)} %param.9, s32[1536]{0:T(1024)S(1)} %broadcast_multiply_fusion), kind=kLoop, calls=%fused_computation | loop fusion | flops 786432 | bytes 2365440 | tf_op jit(solution)/shard_map/convert_element_type | solution.py:318
  3.7 0.7 copy.16
  4.4 0.0 copy-start.4
  4.4 0.0 copy-start.5
  4.4 0.2 reshape.49
  4.6 1.2 %reshape.50.seg_ref = s16[32,16,768]{2,1,0:T(8,128)(2,1)} reshape(s16[32,8,2,768]{3,2,1,0:T(2,128)(2,1)S(1)} %bitcast.52) | data formatting | bytes 1572864 | tf_op jit(solution)/shard_map/reshape | solution.py:319
  5.8 0.0 copy-done.4
  5.8 0.0 copy-done.5
  5.8 0.6 pad_maximum_fusion.1.v_ref
  6.5 0.0 copy-start.3
  6.5 55.8 %shard_map.112 = f32[512,256]{1,0:T(8,128)} custom-call(s16[32,16,768]{2,1,0:T(8,128)(2,1)} %reshape.50.seg_ref, bf16[32,1536]{1,0:T(8,128)(2,1)} %pad_maximum_fusion.1.v_ref), custom_call_target="tpu_custom_call" | custom-call | flops 12884901888 | bytes 4456448 | tf_op jit(solution)/shard_map/pallas_call | solution.py:286
  62.3 0.0 copy-start.1
  62.3 0.0 copy-done.3
  62.3 0.0 copy-start.2
  62.3 1.2 %select_bitcast_fusion.1 = (f32[2,8,1,16,256]{4,3,2,1,0:T(8,128)S(1)}, f32[2,8,1,16,256]{4,3,2,1,0:T(8,128)S(1)}) fusion(pred[8]{0:T(512)(128)(4,1)S(1)} %get-tuple-element.10, f32[2,8,16,256]{3,2,1,0:T(8,128)S(1)} %copy-done.3, f32[2,8,2,16,256]{4,3,2,1,0:T(8,128)} %bitcast.55, pred[8]{0:T(512)(128)(4,1)S(1)} %get-tuple-element.9), kind=kLoop, calls=%fused_computation.7 | loop fusion | flops 393216 | bytes 1310736 | tf_op jit(solution)/shard_map/stack | solution.py:331
  63.6 0.0 copy-start
  63.6 0.0 copy-done.1
  63.6 0.6 fusion.1
  64.2 0.0 copy-done.2
  64.2 0.6 fusion.2
  64.8 0.8 bitcast_reduce_fusion.p_ref
  65.6 0.0 copy-done
  65.6 21.2 %shard_map.113 = (f32[16,256]{1,0:T(8,128)}, f32[16,128]{1,0:T(8,128)}) custom-call(f32[16,256]{1,0:T(8,128)} %bitcast_reduce_fusion.p_ref), custom_call_target="tpu_custom_call" | custom-call | tf_op jit(solution)/shard_map/pallas_call | solution.py:140
  86.8 1.3 %slice_reduce_fusion = f32[16]{0:T(128)} fusion(f32[16,128]{1,0:T(8,128)} %get-tuple-element.6), kind=kLoop, calls=%fused_computation.11 | loop fusion | bytes 128 | tf_op jit(solution)/shard_map/slice | solution.py:334
  88.1 1.3 %copy.23 = f32[16,256]{1,0:T(8,128)} copy(f32[16,256]{1,0:T(8,128)} %get-tuple-element.15) | data formatting | bytes 32768
  (1 shorter events, 0.0 us)
Async XLA Ops:
  4.4 1.5 %copy-start.4 = (bf16[1536,16]{0,1:T(8,128)(2,1)S(1)}, bf16[1536,16]{0,1:T(8,128)(2,1)}, u32[]{:S(2)}) copy-start(bf16[1536,16]{0,1:T(8,128)(2,1)} %param.12) | copy-start | bytes 147460
  4.4 1.4 %copy-start.5 = (bf16[1536,16]{0,1:T(8,128)(2,1)S(1)}, bf16[1536,16]{0,1:T(8,128)(2,1)}, u32[]{:S(2)}) copy-start(bf16[1536,16]{0,1:T(8,128)(2,1)} %param.11) | copy-start | bytes 147460
  6.5 55.8 %copy-start.3 = (f32[2,8,16,256]{3,2,1,0:T(8,128)S(1)}, f32[2,8,16,256]{3,2,1,0:T(8,128)}, u32[]{:S(2)}) copy-start(f32[2,8,16,256]{3,2,1,0:T(8,128)} %param.15) | copy-start | bytes 786436
  62.3 1.3 %copy-start.1 = (f32[256,256]{1,0:T(8,128)S(1)}, f32[256,256]{1,0:T(8,128)}, u32[]{:S(2)}) copy-start(f32[256,256]{1,0:T(8,128)} %constant.6.clone) | copy-start | bytes 786436
  62.3 1.9 %copy-start.2 = (f32[256,256]{1,0:T(8,128)S(1)}, f32[256,256]{1,0:T(8,128)}, u32[]{:S(2)}) copy-start(f32[256,256]{1,0:T(8,128)} %constant.16.clone) | copy-start | bytes 786436
  63.6 2.0 %copy-start = (f32[2,8,2,16,256]{4,3,2,1,0:T(8,128)}, f32[2,8,2,16,256]{4,3,2,1,0:T(8,128)S(1)}, u32[]{:S(2)}) copy-start(f32[2,8,2,16,256]{4,3,2,1,0:T(8,128)S(1)} %pad_maximum_fusion) | copy-start | bytes 1572868

commit v6 on v5

--- a/solution.py
+++ b/solution.py
@@ -9,35 +9,6 @@
 from jax.sharding import PartitionSpec as P
 
 BINS = 32
-
-
-def prefix_matrices(span):
-    i = np.arange(span)[:, None]
-    j = np.arange(span)[None, :]
-    same = (i // BINS) == (j // BINS)
-    tri = (same & (i <= j)).astype(np.float32)
-    last = (i == (j // BINS) * BINS + BINS - 1).astype(np.float32)
-    return jnp.asarray(tri), jnp.asarray(last)
-
-
-def gain_terms(node_hist):
-    _, nodes, targets, span = node_hist.shape
-    tri, last = prefix_matrices(span)
-    flat = node_hist.reshape(2 * nodes * targets, span)
-    left = jnp.dot(flat, tri, precision=lax.Precision.HIGHEST, preferred_element_type=jnp.float32)
-    total = jnp.dot(left, last, precision=lax.Precision.HIGHEST, preferred_element_type=jnp.float32)
-    left = left.reshape(2, nodes, targets, span)
-    total = total.reshape(2, nodes, targets, span)
-    left_g, left_h = left[0], left[1]
-    total_g, total_h = total[0], total[1]
-
-    def score(a, s):
-        return a * a / (jnp.maximum(s, 0.0) + 1.0)
-
-    gain = (
-        score(left_g, left_h) + score(total_g - left_g, total_h - left_h) - score(total_g, total_h)
-    )
-    return jnp.sum(gain, axis=1)
 
 
 MESH_ID = pl.DeviceIdType.MESH
@@ -63,22 +34,16 @@
     return [peer for stage in row_stages(r, n_rows) for peer in stage]
 
 
-def exchange_kernel(p_ref, split_ref, best_ref, gbuf, mbuf, gsend, grecv, msend, mrecv, *, targets):
+def exchange(partial, split_ref, best_ref, gbuf, mbuf, gsend, grecv, msend, mrecv, targets):
     n_rows = lax.axis_size("rows")
     n_outs = lax.axis_size("outs")
     r = lax.axis_index("rows")
     o = lax.axis_index("outs")
-    barrier = pltpu.get_barrier_semaphore()
-    for k in range(1, n_outs):
-        pl.semaphore_signal(barrier, 1, device_id=(r, (o + k) % n_outs), device_id_type=MESH_ID)
-    for peer in row_peers(r, n_rows):
-        pl.semaphore_signal(barrier, 1, device_id=(peer, o), device_id_type=MESH_ID)
-    pl.semaphore_wait(barrier, n_outs - 1 + len(row_peers(r, n_rows)))
-
+    gbuf[o] = partial
     sends = []
     for k in range(1, n_outs):
         copy = pltpu.make_async_remote_copy(
-            src_ref=p_ref,
+            src_ref=gbuf.at[o],
             dst_ref=gbuf.at[o],
             send_sem=gsend.at[k],
             recv_sem=grecv.at[o],
@@ -87,11 +52,10 @@
         )
         copy.start()
         sends.append(copy)
-    gbuf[o] = p_ref[...]
     for k in range(1, n_outs):
         src = (o + n_outs - k) % n_outs
         pltpu.make_async_remote_copy(
-            src_ref=p_ref,
+            src_ref=gbuf.at[o],
             dst_ref=gbuf.at[src],
             send_sem=gsend.at[k],
             recv_sem=grecv.at[src],
@@ -132,31 +96,6 @@
     best_ref[...] = best
 
 
-def exchange_gains(partial_gain, targets):
-    nodes, span = partial_gain.shape
-    n_rows = lax.axis_size("rows")
-    n_outs = lax.axis_size("outs")
-    width = 128
-    return pl.pallas_call(
-        functools.partial(exchange_kernel, targets=targets),
-        out_shape=(
-            jax.ShapeDtypeStruct((nodes, span), jnp.float32),
-            jax.ShapeDtypeStruct((nodes, width), jnp.float32),
-        ),
-        in_specs=[pl.BlockSpec(memory_space=pltpu.VMEM)],
-        out_specs=(pl.BlockSpec(memory_space=pltpu.VMEM), pl.BlockSpec(memory_space=pltpu.VMEM)),
-        scratch_shapes=[
-            pltpu.VMEM((n_outs, nodes, span), jnp.float32),
-            pltpu.VMEM((n_rows, nodes, width), jnp.float32),
-            pltpu.SemaphoreType.DMA((n_outs,)),
-            pltpu.SemaphoreType.DMA((n_outs,)),
-            pltpu.SemaphoreType.DMA((n_rows,)),
-            pltpu.SemaphoreType.DMA((n_rows,)),
-        ],
-        compiler_params=pltpu.CompilerParams(collective_id=0, has_side_effects=True),
-    )(partial_gain)
-
-
 def block_hist(acc_ref, v, s, nodes):
     tl = v.shape[0] // 2
     half = s.shape[1]
@@ -182,7 +121,11 @@
         )
 
 
-def gather_hist_kernel(seg_ref, v_ref, acc_ref, vbuf, sbuf, vsend, fsend, vrecv, ssend, srecv, *, nodes):
+def gather_hist_kernel(
+    small_ref, evict_ref, seg_ref, v_ref, parent_ref, hist_ref, split_ref, best_ref,
+    acc_ref, vbuf, sbuf, vsend, fsend, vrecv, ssend, srecv, gbuf, mbuf, gsend, grecv, msend, mrecv,
+    *, nodes, targets,
+):
     n_rows = lax.axis_size("rows")
     chips = n_rows // 2
     r = lax.axis_index("rows")
@@ -197,7 +140,10 @@
         return carry
 
     lax.fori_loop(1, n_rows, greet, 0)
-    pl.semaphore_wait(barrier, n_rows - 1)
+    n_outs = lax.axis_size("outs")
+    for k in range(1, n_outs):
+        pl.semaphore_signal(barrier, 1, device_id=(r, (o + k) % n_outs), device_id_type=MESH_ID)
+    pl.semaphore_wait(barrier, n_rows - 1 + n_outs - 1)
 
     def s_copy(k, peer, slot):
         return pltpu.make_async_remote_copy(
@@ -275,25 +221,96 @@
 
     lax.fori_loop(1, chips, drain_f, 0)
 
-
-def gather_hist(seg_p, v_loc, nodes):
+    node_hist(acc_ref, parent_ref, small_ref, evict_ref, hist_ref, nodes)
+    partial = gain_terms(hist_ref, nodes)
+    exchange(partial, split_ref, best_ref, gbuf, mbuf, gsend, grecv, msend, mrecv, targets)
+
+
+def node_hist(acc_ref, parent_ref, small_ref, evict_ref, hist_ref, nodes):
+    pairs = nodes // 2
+    tl = acc_ref.shape[0] // (2 * nodes)
+    for c in range(2):
+        for p in range(pairs):
+            lo = c * nodes * tl + 2 * p * tl
+            a = acc_ref[lo : lo + tl]
+            b = acc_ref[lo + tl : lo + 2 * tl]
+            base = (c * pairs + p) * tl
+            parent = parent_ref[base : base + tl]
+            small = small_ref[p] == 0
+            gone = evict_ref[p] == 1
+            child = jnp.where(small, a, b)
+            rebuilt = jnp.where(small, b, a)
+            sibling = jnp.where(gone, rebuilt, parent - child)
+            hist_ref[lo : lo + tl] = jnp.where(small, child, sibling)
+            hist_ref[lo + tl : lo + 2 * tl] = jnp.where(small, sibling, child)
+
+
+def group_scan(x, reverse):
+    span = x.shape[1]
+    lane = lax.broadcasted_iota(jnp.int32, x.shape, 1) % BINS
+    shift = 1
+    while shift < BINS:
+        if reverse:
+            moved = pltpu.roll(x, span - shift, 1)
+            x = x + jnp.where(lane + shift < BINS, moved, 0.0)
+        else:
+            moved = pltpu.roll(x, shift, 1)
+            x = x + jnp.where(lane >= shift, moved, 0.0)
+        shift *= 2
+    return x
+
+
+def gain_terms(hist_ref, nodes):
+    rows, span = hist_ref.shape
+    half = rows // 2
+    tl = half // nodes
+    lane = lax.broadcasted_iota(jnp.int32, (half, span), 1) % BINS
+    left_g = group_scan(hist_ref[0:half], False)
+    left_h = group_scan(hist_ref[half:rows], False)
+    total_g = group_scan(jnp.where(lane == BINS - 1, left_g, 0.0), True)
+    total_h = group_scan(jnp.where(lane == BINS - 1, left_h, 0.0), True)
+
+    def score(a, s):
+        return a * a / (jnp.maximum(s, 0.0) + 1.0)
+
+    gain = (
+        score(left_g, left_h) + score(total_g - left_g, total_h - left_h) - score(total_g, total_h)
+    )
+    return jnp.sum(gain.reshape(nodes, tl, span), axis=1)
+
+
+def gather_hist(small_side, evicted, seg_p, v_loc, parent, nodes, targets):
     n_rows, width, half = seg_p.shape
+    n_outs = lax.axis_size("outs")
     vw, rows = v_loc.shape
     feats = width // 2
     out_rows = vw * nodes
     cols = feats * BINS
     total = n_rows * rows
+    vmem = pl.BlockSpec(memory_space=pltpu.VMEM)
+    smem = pl.BlockSpec(memory_space=pltpu.SMEM)
     return pl.pallas_call(
-        functools.partial(gather_hist_kernel, nodes=nodes),
-        out_shape=jax.ShapeDtypeStruct((out_rows, cols), jnp.float32),
-        in_specs=[pl.BlockSpec(memory_space=pltpu.VMEM)] * 2,
-        out_specs=pl.BlockSpec(memory_space=pltpu.VMEM),
+        functools.partial(gather_hist_kernel, nodes=nodes, targets=targets),
+        out_shape=(
+            jax.ShapeDtypeStruct((out_rows, cols), jnp.float32),
+            jax.ShapeDtypeStruct((nodes, cols), jnp.float32),
+            jax.ShapeDtypeStruct((nodes, 128), jnp.float32),
+        ),
+        in_specs=[smem, smem, vmem, vmem, vmem],
+        out_specs=(vmem, vmem, vmem),
         scratch_shapes=[
+            pltpu.VMEM((out_rows, cols), jnp.float32),
             pltpu.VMEM((n_rows, vw, rows), v_loc.dtype),
             pltpu.VMEM((n_rows, width, half), seg_p.dtype),
             pltpu.SemaphoreType.DMA((n_rows // 2,)),
             pltpu.SemaphoreType.DMA((n_rows // 2,)),
             pltpu.SemaphoreType.DMA((n_rows,)),
+            pltpu.SemaphoreType.DMA((n_rows,)),
+            pltpu.SemaphoreType.DMA((n_rows,)),
+            pltpu.VMEM((n_outs, nodes, cols), jnp.float32),
+            pltpu.VMEM((n_rows, nodes, 128), jnp.float32),
+            pltpu.SemaphoreType.DMA((n_outs,)),
+            pltpu.SemaphoreType.DMA((n_outs,)),
             pltpu.SemaphoreType.DMA((n_rows,)),
             pltpu.SemaphoreType.DMA((n_rows,)),
         ],
@@ -303,7 +320,7 @@
             bytes_accessed=total * (vw * 2 + feats * 2) + out_rows * cols * 4,
             transcendentals=0,
         ),
-    )(seg_p, v_loc)
+    )(small_side, evicted, seg_p, v_loc, parent)
 
 
 def local(codes, node_of_row, grad, hess, small_side, evicted, parent_hist):
@@ -319,20 +336,10 @@
     seg_p = jnp.transpose(seg.reshape(2, half, n_rows, feats), (2, 3, 0, 1)).reshape(n_rows, 2 * feats, half)
     v_loc = jnp.concatenate([grad.T, hess.T], axis=0)
     span = feats * BINS
-    built = gather_hist(seg_p, v_loc, nodes).reshape(2, nodes, local_targets, span)
-    small = (small_side == 0)[None, :, None, None]
-    pair_view = built.reshape(2, pairs, 2, local_targets, span)
-    child = jnp.where(small, pair_view[:, :, 0], pair_view[:, :, 1])
-    rebuilt = jnp.where(small, pair_view[:, :, 1], pair_view[:, :, 0])
-    gone = (evicted == 1)[None, :, None, None]
-    sibling = jnp.where(gone, rebuilt, parent_hist - child)
-    first = jnp.where(small, child, sibling)
-    second = jnp.where(small, sibling, child)
-    node_hist = jnp.stack([first, second], axis=2).reshape(2, nodes, local_targets, span)
-    partial_gain = gain_terms(node_hist)
-    split_gain, best = exchange_gains(partial_gain, targets)
-    best_gain = best[:, 0]
-    return (node_hist, split_gain, best_gain)
+    parent = parent_hist.reshape(2 * pairs * local_targets, span)
+    hist, split_gain, best = gather_hist(small_side, evicted, seg_p, v_loc, parent, nodes, targets)
+    node_hist = hist.reshape(2, nodes, local_targets, span)
+    return (node_hist, split_gain, best[:, 0])
 
 
 def solution(mesh):

time: 89.9 us -> 86.1 us (0.958)
  other arithmetic: 5.76 us -> 3.02 us
  Pallas kernels: 77 us -> 74.5 us
  local copies, waits for them, and re-layouts: 4.78 us -> 6.62 us
  matrix products: 1.16 us -> 0 us
    pallas_call x2 -> x1, Pallas kernels: 77 us -> 74.5 us  [gather_hist(): pl.pallas_call(functools.partial(gather_hist_kernel, nodes=nodes, targets...]
    unnamed x13 -> x6, local copies, waits for them, and re-layouts: 1.36 us -> 3.2 us
    another operation x2 -> x0, other arithmetic: 1.25 us -> none  [local(): jnp.stack([first, second], axis=2).reshape(2, nodes, local_targets, span)]
    dot_general x2 -> x0, matrix products: 1.16 us -> none  [the longest x1 0.58 us: gain_terms(): jnp.dot(left, last, precision=lax.Precision.HIGHEST, preferred_element_ty...]
where the time goes in v6:
time: 86.1 us; the launch traced here: 84.9 us
  Pallas kernels  74.5 us (87%)
  local copies, waits for them, and re-layouts  6.62 us (8%)
  other arithmetic  3.02 us (4%)
    pallas_call x1, Pallas kernels, gather_hist(): pl.pallas_call(functools.partial(gather_hist_kernel, nodes=nodes, targets...  74.5 us
    unnamed x6, local copies, waits for them, and re-layouts  3.2 us

profile of v6, /device:TPU:1, one launch (start us, length us, event | category | flops | bytes accessed | tf_op | source)
XLA Modules:
  0.0 84.9 jit_solution(3436236471231759009)
XLA Ops:
  0.6 0.7 broadcast_multiply_fusion
  1.3 1.7 %add_convert_fusion = s16[1536,256]{1,0:T(8,128)(2,1)S(1)} fusion(s32[1536,256]{1,0:T(8,128)} %param.7, s32[1536]{0:T(1024)S(1)} %broadcast_multiply_fusion), kind=kLoop, calls=%fused_computation | loop fusion | flops 786432 | bytes 2365440 | tf_op jit(solution)/shard_map/convert_element_type | solution.py:335
  3.0 0.7 copy.11
  3.7 0.0 copy-start
  3.7 0.0 copy-start.1
  3.7 0.2 reshape.20
  3.9 1.2 %reshape.21.seg_ref = s16[32,16,768]{2,1,0:T(8,128)(2,1)} reshape(s16[32,8,2,768]{3,2,1,0:T(2,128)(2,1)S(1)} %bitcast.7) | data formatting | bytes 1572864 | tf_op jit(solution)/shard_map/reshape | solution.py:336
  5.1 0.0 copy-done
  5.1 0.0 copy-done.1
  5.1 0.6 pad_maximum_fusion.v_ref
  5.8 74.5 %shard_map.94 = (f32[512,256]{1,0:T(8,128)}, f32[16,256]{1,0:T(8,128)}, f32[16,128]{1,0:T(8,128)}) custom-call(s32[8]{0:T(128)} %small_ref.1, s32[8]{0:T(128)} %evict_ref.1, s16[32,16,768]{2,1,0:T(8,128)(2,1)} %reshape.21.seg_ref, bf16[32,1536]{1,0:T(8,128)(2,1)} %pad_maximum_fusion.v_ref, f32[256,256]{1,0:T(8,128)} %bitcast.11), custom_call_target="tpu_custom_call" | custom-call | flops 12884901888 | bytes 4456448 | tf_op jit(solution)/shard_map/pallas_call | solution.py:292
  80.3 1.3 %slice_reduce_fusion = f32[16]{0:T(128)} fusion(f32[16,128]{1,0:T(8,128)} %get-tuple-element.8), kind=kLoop, calls=%fused_computation.2 | loop fusion | bytes 128 | tf_op jit(solution)/shard_map/slice | solution.py:342
  81.7 1.9 %copy.14 = f32[2,16,16,256]{3,2,1,0:T(8,128)} copy(f32[2,16,16,256]{3,2,1,0:T(8,128)} %bitcast.8) | data formatting | bytes 1048576
  83.5 1.3 %copy.15 = f32[16,256]{1,0:T(8,128)} copy(f32[16,256]{1,0:T(8,128)} %get-tuple-element.13) | data formatting | bytes 32768
Async XLA Ops:
  3.7 1.5 %copy-start = (bf16[1536,16]{0,1:T(8,128)(2,1)S(1)}, bf16[1536,16]{0,1:T(8,128)(2,1)}, u32[]{:S(2)}) copy-start(bf16[1536,16]{0,1:T(8,128)(2,1)} %param.10) | copy-start | bytes 147460
  3.7 1.4 %copy-start.1 = (bf16[1536,16]{0,1:T(8,128)(2,1)S(1)}, bf16[1536,16]{0,1:T(8,128)(2,1)}, u32[]{:S(2)}) copy-start(bf16[1536,16]{0,1:T(8,128)(2,1)} %param.9) | copy-start | bytes 147460

commit v7 on v6

--- a/solution.py
+++ b/solution.py
@@ -22,9 +22,9 @@
     core = r % 2
     y = chip // nx
     x = chip % nx
+    row = 2 * nx
     stages = [
-        [chip * 2 + 1 - core],
-        [(y * nx + (x + k) % nx) * 2 + core for k in range(1, nx)],
+        [y * row + (r - y * row + k) % row for k in range(1, row)],
         [(((y + k) % ny) * nx + x) * 2 + core for k in range(1, ny)],
     ]
     return [stage for stage in stages if stage]
@@ -143,6 +143,8 @@
     n_outs = lax.axis_size("outs")
     for k in range(1, n_outs):
         pl.semaphore_signal(barrier, 1, device_id=(r, (o + k) % n_outs), device_id_type=MESH_ID)
+    acc_ref[...] = jnp.zeros_like(acc_ref)
+    block_hist(acc_ref, v_ref[...], seg_ref[r].astype(jnp.int32), nodes)
     pl.semaphore_wait(barrier, n_rows - 1 + n_outs - 1)
 
     def s_copy(k, peer, slot):
@@ -180,8 +182,6 @@
         return carry
 
     lax.fori_loop(1, n_rows, send_seg, 0)
-    acc_ref[...] = jnp.zeros_like(acc_ref)
-    block_hist(acc_ref, v_ref[...], seg_ref[r].astype(jnp.int32), nodes)
 
     def take_direct(k, carry):
         src = ((chip + chips - k) % chips) * 2 + core

time: 86.1 us -> 85.3 us (level)
  no operation moved by 1% of the time
where the time goes in v7:
time: 85.3 us; the launch traced here: 84.4 us
  Pallas kernels  74 us (87%)
  local copies, waits for them, and re-layouts  6.62 us (8%)
  other arithmetic  3.02 us (4%)
    pallas_call x1, Pallas kernels, gather_hist(): pl.pallas_call(functools.partial(gather_hist_kernel, nodes=nodes, targets...  74 us
    unnamed x6, local copies, waits for them, and re-layouts  3.2 us

profile of v7, /device:TPU:1, one launch (start us, length us, event | category | flops | bytes accessed | tf_op | source)
XLA Modules:
  0.0 84.4 jit_solution(1156422712066807419)
XLA Ops:
  0.6 0.7 broadcast_multiply_fusion
  1.3 1.7 %add_convert_fusion = s16[1536,256]{1,0:T(8,128)(2,1)S(1)} fusion(s32[1536,256]{1,0:T(8,128)} %param.7, s32[1536]{0:T(1024)S(1)} %broadcast_multiply_fusion), kind=kLoop, calls=%fused_computation | loop fusion | flops 786432 | bytes 2365440 | tf_op jit(solution)/shard_map/convert_element_type | solution.py:335
  3.0 0.7 copy.11
  3.7 0.0 copy-start
  3.7 0.0 copy-start.1
  3.7 0.2 reshape.20
  3.9 1.2 %reshape.21.seg_ref = s16[32,16,768]{2,1,0:T(8,128)(2,1)} reshape(s16[32,8,2,768]{3,2,1,0:T(2,128)(2,1)S(1)} %bitcast.7) | data formatting | bytes 1572864 | tf_op jit(solution)/shard_map/reshape | solution.py:336
  5.1 0.0 copy-done
  5.1 0.0 copy-done.1
  5.1 0.6 pad_maximum_fusion.v_ref
  5.8 74.0 %shard_map.94 = (f32[512,256]{1,0:T(8,128)}, f32[16,256]{1,0:T(8,128)}, f32[16,128]{1,0:T(8,128)}) custom-call(s32[8]{0:T(128)} %small_ref.1, s32[8]{0:T(128)} %evict_ref.1, s16[32,16,768]{2,1,0:T(8,128)(2,1)} %reshape.21.seg_ref, bf16[32,1536]{1,0:T(8,128)(2,1)} %pad_maximum_fusion.v_ref, f32[256,256]{1,0:T(8,128)} %bitcast.11), custom_call_target="tpu_custom_call" | custom-call | flops 12884901888 | bytes 4456448 | tf_op jit(solution)/shard_map/pallas_call | solution.py:292
  79.8 1.3 %slice_reduce_fusion = f32[16]{0:T(128)} fusion(f32[16,128]{1,0:T(8,128)} %get-tuple-element.8), kind=kLoop, calls=%fused_computation.2 | loop fusion | bytes 128 | tf_op jit(solution)/shard_map/slice | solution.py:342
  81.2 1.9 %copy.14 = f32[2,16,16,256]{3,2,1,0:T(8,128)} copy(f32[2,16,16,256]{3,2,1,0:T(8,128)} %bitcast.8) | data formatting | bytes 1048576
  83.0 1.3 %copy.15 = f32[16,256]{1,0:T(8,128)} copy(f32[16,256]{1,0:T(8,128)} %get-tuple-element.13) | data formatting | bytes 32768
Async XLA Ops:
  3.7 1.5 %copy-start = (bf16[1536,16]{0,1:T(8,128)(2,1)S(1)}, bf16[1536,16]{0,1:T(8,128)(2,1)}, u32[]{:S(2)}) copy-start(bf16[1536,16]{0,1:T(8,128)(2,1)} %param.10) | copy-start | bytes 147460
  3.7 1.4 %copy-start.1 = (bf16[1536,16]{0,1:T(8,128)(2,1)S(1)}, bf16[1536,16]{0,1:T(8,128)(2,1)}, u32[]{:S(2)}) copy-start(bf16[1536,16]{0,1:T(8,128)(2,1)} %param.9) | copy-start | bytes 147460

commit v8 on v7

--- a/solution.py
+++ b/solution.py
@@ -183,24 +183,23 @@
 
     lax.fori_loop(1, n_rows, send_seg, 0)
 
-    def take_direct(k, carry):
+    def take_forwarded(k):
+        src = ((chip + chips - k) % chips) * 2 + 1 - core
+        f_copy(k, src).wait_recv()
+        s_copy(k, src, src).wait_recv()
+        block_hist(acc_ref, vbuf[src], sbuf[src].astype(jnp.int32), nodes)
+
+    def take(k, carry):
         src = ((chip + chips - k) % chips) * 2 + core
         v_copy(k, src, src).wait_recv()
         f_copy(k, src).start()
         s_copy(k, src, src).wait_recv()
         block_hist(acc_ref, vbuf[src], sbuf[src].astype(jnp.int32), nodes)
-        return carry
-
-    lax.fori_loop(1, chips, take_direct, 0)
-
-    def take_forwarded(k, carry):
-        src = ((chip + chips - k) % chips) * 2 + 1 - core
-        f_copy(k, src).wait_recv()
-        s_copy(k, src, src).wait_recv()
-        block_hist(acc_ref, vbuf[src], sbuf[src].astype(jnp.int32), nodes)
-        return carry
-
-    lax.fori_loop(0, chips, take_forwarded, 0)
+        take_forwarded(k)
+        return carry
+
+    take_forwarded(0)
+    lax.fori_loop(1, chips, take, 0)
 
     def drain(k, carry):
         s_copy(k, (r + k) % n_rows, r).wait_send()

time: 85.3 us -> 96.8 us (1.13)
  Pallas kernels: 74 us -> 85.1 us
    pallas_call x1, Pallas kernels: 74 us -> 85.1 us  [gather_hist(): pl.pallas_call(functools.partial(gather_hist_kernel, nodes=nodes, targets...]
where the time goes in v8:
time: 96.8 us; the launch traced here: 95.4 us
  Pallas kernels  85.1 us (88%)
  local copies, waits for them, and re-layouts  6.62 us (7%)
  other arithmetic  3.02 us (3%)
    pallas_call x1, Pallas kernels, gather_hist(): pl.pallas_call(functools.partial(gather_hist_kernel, nodes=nodes, targets...  85.1 us
    unnamed x6, local copies, waits for them, and re-layouts  3.2 us

profile of v8, /device:TPU:1, one launch (start us, length us, event | category | flops | bytes accessed | tf_op | source)
XLA Modules:
  0.0 95.4 jit_solution(1722207694164765187)
XLA Ops:
  0.6 0.7 broadcast_multiply_fusion
  1.3 1.7 %add_convert_fusion = s16[1536,256]{1,0:T(8,128)(2,1)S(1)} fusion(s32[1536,256]{1,0:T(8,128)} %param.7, s32[1536]{0:T(1024)S(1)} %broadcast_multiply_fusion), kind=kLoop, calls=%fused_computation | loop fusion | flops 786432 | bytes 2365440 | tf_op jit(solution)/shard_map/convert_element_type | solution.py:334
  3.0 0.7 copy.11
  3.7 0.0 copy-start
  3.7 0.0 copy-start.1
  3.7 0.2 reshape.20
  3.9 1.2 %reshape.21.seg_ref = s16[32,16,768]{2,1,0:T(8,128)(2,1)} reshape(s16[32,8,2,768]{3,2,1,0:T(2,128)(2,1)S(1)} %bitcast.7) | data formatting | bytes 1572864 | tf_op jit(solution)/shard_map/reshape | solution.py:335
  5.1 0.0 copy-done
  5.1 0.0 copy-done.1
  5.1 0.6 pad_maximum_fusion.v_ref
  5.8 85.1 %shard_map.94 = (f32[512,256]{1,0:T(8,128)}, f32[16,256]{1,0:T(8,128)}, f32[16,128]{1,0:T(8,128)}) custom-call(s32[8]{0:T(128)} %small_ref.1, s32[8]{0:T(128)} %evict_ref.1, s16[32,16,768]{2,1,0:T(8,128)(2,1)} %reshape.21.seg_ref, bf16[32,1536]{1,0:T(8,128)(2,1)} %pad_maximum_fusion.v_ref, f32[256,256]{1,0:T(8,128)} %bitcast.11), custom_call_target="tpu_custom_call" | custom-call | flops 12884901888 | bytes 4456448 | tf_op jit(solution)/shard_map/pallas_call | solution.py:291
  90.9 1.3 %slice_reduce_fusion = f32[16]{0:T(128)} fusion(f32[16,128]{1,0:T(8,128)} %get-tuple-element.8), kind=kLoop, calls=%fused_computation.2 | loop fusion | bytes 128 | tf_op jit(solution)/shard_map/slice | solution.py:341
  92.2 1.9 %copy.14 = f32[2,16,16,256]{3,2,1,0:T(8,128)} copy(f32[2,16,16,256]{3,2,1,0:T(8,128)} %bitcast.8) | data formatting | bytes 1048576
  94.1 1.3 %copy.15 = f32[16,256]{1,0:T(8,128)} copy(f32[16,256]{1,0:T(8,128)} %get-tuple-element.13) | data formatting | bytes 32768
Async XLA Ops:
  3.7 1.5 %copy-start = (bf16[1536,16]{0,1:T(8,128)(2,1)S(1)}, bf16[1536,16]{0,1:T(8,128)(2,1)}, u32[]{:S(2)}) copy-start(bf16[1536,16]{0,1:T(8,128)(2,1)} %param.10) | copy-start | bytes 147460
  3.7 1.4 %copy-start.1 = (bf16[1536,16]{0,1:T(8,128)(2,1)S(1)}, bf16[1536,16]{0,1:T(8,128)(2,1)}, u32[]{:S(2)}) copy-start(bf16[1536,16]{0,1:T(8,128)(2,1)} %param.9) | copy-start | bytes 147460

commit v9 on v8

--- a/solution.py
+++ b/solution.py
@@ -9,6 +9,7 @@
 from jax.sharding import PartitionSpec as P
 
 BINS = 32
+LAG = 3
 
 
 MESH_ID = pl.DeviceIdType.MESH
@@ -189,17 +190,30 @@
         s_copy(k, src, src).wait_recv()
         block_hist(acc_ref, vbuf[src], sbuf[src].astype(jnp.int32), nodes)
 
-    def take(k, carry):
+    def take_direct(k):
         src = ((chip + chips - k) % chips) * 2 + core
         v_copy(k, src, src).wait_recv()
         f_copy(k, src).start()
         s_copy(k, src, src).wait_recv()
         block_hist(acc_ref, vbuf[src], sbuf[src].astype(jnp.int32), nodes)
+
+    def lead(k, carry):
+        take_direct(k)
+        return carry
+
+    def take(k, carry):
+        take_direct(k)
+        take_forwarded(k - LAG)
+        return carry
+
+    def tail(k, carry):
         take_forwarded(k)
         return carry
 
-    take_forwarded(0)
-    lax.fori_loop(1, chips, take, 0)
+    lag = min(LAG, chips)
+    lax.fori_loop(1, lag, lead, 0)
+    lax.fori_loop(lag, chips, take, 0)
+    lax.fori_loop(chips - lag, chips, tail, 0)
 
     def drain(k, carry):
         s_copy(k, (r + k) % n_rows, r).wait_send()

time: 96.8 us -> 94.5 us (0.976)
  Pallas kernels: 85.1 us -> 83.2 us
    pallas_call x1, Pallas kernels: 85.1 us -> 83.2 us  [gather_hist(): pl.pallas_call(functools.partial(gather_hist_kernel, nodes=nodes, targets...]
where the time goes in v9:
time: 94.5 us; the launch traced here: 93.5 us
  Pallas kernels  83.2 us (88%)
  local copies, waits for them, and re-layouts  6.62 us (7%)
  other arithmetic  3.02 us (3%)
    pallas_call x1, Pallas kernels, gather_hist(): pl.pallas_call(functools.partial(gather_hist_kernel, nodes=nodes, targets...  83.2 us
    unnamed x6, local copies, waits for them, and re-layouts  3.2 us

profile of v9, /device:TPU:1, one launch (start us, length us, event | category | flops | bytes accessed | tf_op | source)
XLA Modules:
  0.0 93.5 jit_solution(18315769578672288494)
XLA Ops:
  0.6 0.7 broadcast_multiply_fusion
  1.3 1.7 %add_convert_fusion = s16[1536,256]{1,0:T(8,128)(2,1)S(1)} fusion(s32[1536,256]{1,0:T(8,128)} %param.7, s32[1536]{0:T(1024)S(1)} %broadcast_multiply_fusion), kind=kLoop, calls=%fused_computation | loop fusion | flops 786432 | bytes 2365440 | tf_op jit(solution)/shard_map/convert_element_type | solution.py:348
  3.0 0.7 copy.11
  3.7 0.0 copy-start
  3.7 0.0 copy-start.1
  3.7 0.2 reshape.20
  3.9 1.2 %reshape.21.seg_ref = s16[32,16,768]{2,1,0:T(8,128)(2,1)} reshape(s16[32,8,2,768]{3,2,1,0:T(2,128)(2,1)S(1)} %bitcast.7) | data formatting | bytes 1572864 | tf_op jit(solution)/shard_map/reshape | solution.py:349
  5.1 0.0 copy-done
  5.1 0.0 copy-done.1
  5.1 0.6 pad_maximum_fusion.v_ref
  5.8 83.2 %shard_map.94 = (f32[512,256]{1,0:T(8,128)}, f32[16,256]{1,0:T(8,128)}, f32[16,128]{1,0:T(8,128)}) custom-call(s32[8]{0:T(128)} %small_ref.1, s32[8]{0:T(128)} %evict_ref.1, s16[32,16,768]{2,1,0:T(8,128)(2,1)} %reshape.21.seg_ref, bf16[32,1536]{1,0:T(8,128)(2,1)} %pad_maximum_fusion.v_ref, f32[256,256]{1,0:T(8,128)} %bitcast.11), custom_call_target="tpu_custom_call" | custom-call | flops 12884901888 | bytes 4456448 | tf_op jit(solution)/shard_map/pallas_call | solution.py:305
  89.0 1.3 %slice_reduce_fusion = f32[16]{0:T(128)} fusion(f32[16,128]{1,0:T(8,128)} %get-tuple-element.8), kind=kLoop, calls=%fused_computation.2 | loop fusion | bytes 128 | tf_op jit(solution)/shard_map/slice | solution.py:355
  90.3 1.9 %copy.14 = f32[2,16,16,256]{3,2,1,0:T(8,128)} copy(f32[2,16,16,256]{3,2,1,0:T(8,128)} %bitcast.8) | data formatting | bytes 1048576
  92.2 1.3 %copy.15 = f32[16,256]{1,0:T(8,128)} copy(f32[16,256]{1,0:T(8,128)} %get-tuple-element.13) | data formatting | bytes 32768
Async XLA Ops:
  3.7 1.5 %copy-start = (bf16[1536,16]{0,1:T(8,128)(2,1)S(1)}, bf16[1536,16]{0,1:T(8,128)(2,1)}, u32[]{:S(2)}) copy-start(bf16[1536,16]{0,1:T(8,128)(2,1)} %param.10) | copy-start | bytes 147460
  3.7 1.4 %copy-start.1 = (bf16[1536,16]{0,1:T(8,128)(2,1)S(1)}, bf16[1536,16]{0,1:T(8,128)(2,1)}, u32[]{:S(2)}) copy-start(bf16[1536,16]{0,1:T(8,128)(2,1)} %param.9) | copy-start | bytes 147460

commit v10 on v8

--- a/solution.py
+++ b/solution.py
@@ -121,6 +121,100 @@
         )
 
 
+def relay_gather(acc_ref, seg_ref, v_ref, vbuf, sbuf, vsend, fsend, vrecv, s_copy, send_seg, nodes):
+    n_rows = lax.axis_size("rows")
+    r = lax.axis_index("rows")
+    o = lax.axis_index("outs")
+    core = r % 2
+    chip = r // 2
+    y = chip // 4
+    x = chip % 4
+    a = x + core * (y - x)
+    b = y + core * (x - y)
+    partner = chip * 2 + 1 - core
+
+    def dev(da, db):
+        ap = (a + da + 4) % 4
+        bp = (b + db + 4) % 4
+        return ((1 - core) * (bp * 4 + ap) + core * (ap * 4 + bp)) * 2 + core
+
+    def copy(src, sem, peer, slot):
+        return pltpu.make_async_remote_copy(
+            src_ref=src, dst_ref=vbuf.at[slot], send_sem=sem, recv_sem=vrecv.at[slot],
+            device_id=(peer, o), device_id_type=MESH_ID,
+        )
+
+    def arrive(slot):
+        copy(vbuf.at[slot], vsend.at[0], partner, slot).wait_recv()
+        s_copy(0, slot, slot).wait_recv()
+
+    def compute(slot):
+        block_hist(acc_ref, vbuf[slot], sbuf[slot].astype(jnp.int32), nodes)
+
+    started = []
+
+    def start(src, sem, peer, slot):
+        c = copy(src, sem, peer, slot)
+        c.start()
+        started.append(c)
+
+    start(v_ref, fsend.at[0], partner, r)
+    for j, (da, db) in enumerate([(1, 0), (-1, 0), (0, 1), (0, -1)]):
+        start(v_ref, vsend.at[j], dev(da, db), r)
+    lax.fori_loop(1, n_rows, send_seg, 0)
+
+    sem = 4
+    for j, da in enumerate([-1, 1, -2]):
+        slot = dev(da, 0)
+        arrive(slot)
+        if da == -1:
+            start(vbuf.at[slot], vsend.at[sem], dev(1, 0), slot)
+            sem += 1
+        start(vbuf.at[slot], vsend.at[sem], dev(0, 1), slot)
+        start(vbuf.at[slot], vsend.at[sem + 1], dev(0, -1), slot)
+        sem += 2
+        start(vbuf.at[slot], fsend.at[1 + j], partner, slot)
+        compute(slot)
+
+    def row_step(db, relay, first):
+        def body(i, carry):
+            slot = dev((i * 3) % 4, db)
+            arrive(slot)
+            if relay:
+                copy(vbuf.at[slot], vsend.at[11 + i], dev(0, 1), slot).start()
+            copy(vbuf.at[slot], fsend.at[first + i], partner, slot).start()
+            compute(slot)
+            return carry
+
+        return body
+
+    def row_drain(db, relay, first):
+        def body(i, carry):
+            slot = dev((i * 3) % 4, db)
+            if relay:
+                copy(vbuf.at[slot], vsend.at[11 + i], dev(0, 1), slot).wait_send()
+            copy(vbuf.at[slot], fsend.at[first + i], partner, slot).wait_send()
+            return carry
+
+        return body
+
+    rows_plan = [(-1, True, 4), (1, False, 8), (-2, False, 12)]
+    for db, relay, first in rows_plan:
+        lax.fori_loop(0, 4, row_step(db, relay, first), 0)
+
+    def take_partner(k, carry):
+        slot = ((chip + 16 - k) % 16) * 2 + 1 - core
+        arrive(slot)
+        compute(slot)
+        return carry
+
+    lax.fori_loop(0, 16, take_partner, 0)
+    for c in started:
+        c.wait_send()
+    for db, relay, first in rows_plan:
+        lax.fori_loop(0, 4, row_drain(db, relay, first), 0)
+
+
 def gather_hist_kernel(
     small_ref, evict_ref, seg_ref, v_ref, parent_ref, hist_ref, split_ref, best_ref,
     acc_ref, vbuf, sbuf, vsend, fsend, vrecv, ssend, srecv, gbuf, mbuf, gsend, grecv, msend, mrecv,
@@ -165,60 +259,66 @@
             device_id=(partner, o), device_id_type=MESH_ID,
         )
 
-    own = pltpu.make_async_remote_copy(
-        src_ref=v_ref, dst_ref=vbuf.at[r], send_sem=fsend.at[0], recv_sem=vrecv.at[r],
-        device_id=(partner, o), device_id_type=MESH_ID,
-    )
-    own.start()
-
-    def send(k, carry):
-        v_copy(k, ((chip + k) % chips) * 2 + core, r).start()
-        return carry
-
-    lax.fori_loop(1, chips, send, 0)
-
     def send_seg(k, carry):
         s_copy(k, (r + k) % n_rows, r).start()
         return carry
 
-    lax.fori_loop(1, n_rows, send_seg, 0)
-
-    def take_forwarded(k):
-        src = ((chip + chips - k) % chips) * 2 + 1 - core
-        f_copy(k, src).wait_recv()
-        s_copy(k, src, src).wait_recv()
-        block_hist(acc_ref, vbuf[src], sbuf[src].astype(jnp.int32), nodes)
-
-    def take(k, carry):
-        src = ((chip + chips - k) % chips) * 2 + core
-        v_copy(k, src, src).wait_recv()
-        f_copy(k, src).start()
-        s_copy(k, src, src).wait_recv()
-        block_hist(acc_ref, vbuf[src], sbuf[src].astype(jnp.int32), nodes)
-        take_forwarded(k)
-        return carry
-
-    take_forwarded(0)
-    lax.fori_loop(1, chips, take, 0)
-
     def drain(k, carry):
         s_copy(k, (r + k) % n_rows, r).wait_send()
         return carry
 
-    lax.fori_loop(1, n_rows, drain, 0)
-
-    def drain_v(k, carry):
-        v_copy(k, ((chip + k) % chips) * 2 + core, r).wait_send()
-        return carry
-
-    lax.fori_loop(1, chips, drain_v, 0)
-    own.wait_send()
-
-    def drain_f(k, carry):
-        f_copy(k, ((chip + chips - k) % chips) * 2 + core).wait_send()
-        return carry
-
-    lax.fori_loop(1, chips, drain_f, 0)
+    if chips == 16:
+        relay_gather(acc_ref, seg_ref, v_ref, vbuf, sbuf, vsend, fsend, vrecv, s_copy, send_seg, nodes)
+        lax.fori_loop(1, n_rows, drain, 0)
+    else:
+        own = pltpu.make_async_remote_copy(
+            src_ref=v_ref, dst_ref=vbuf.at[r], send_sem=fsend.at[0], recv_sem=vrecv.at[r],
+            device_id=(partner, o), device_id_type=MESH_ID,
+        )
+        own.start()
+
+        def send(k, carry):
+            v_copy(k, ((chip + k) % chips) * 2 + core, r).start()
+            return carry
+
+        lax.fori_loop(1, chips, send, 0)
+
+        lax.fori_loop(1, n_rows, send_seg, 0)
+
+        def take_direct(k, carry):
+            src = ((chip + chips - k) % chips) * 2 + core
+            v_copy(k, src, src).wait_recv()
+            f_copy(k, src).start()
+            s_copy(k, src, src).wait_recv()
+            block_hist(acc_ref, vbuf[src], sbuf[src].astype(jnp.int32), nodes)
+            return carry
+
+        lax.fori_loop(1, chips, take_direct, 0)
+
+        def take_forwarded(k, carry):
+            src = ((chip + chips - k) % chips) * 2 + 1 - core
+            f_copy(k, src).wait_recv()
+            s_copy(k, src, src).wait_recv()
+            block_hist(acc_ref, vbuf[src], sbuf[src].astype(jnp.int32), nodes)
+            return carry
+
+        lax.fori_loop(0, chips, take_forwarded, 0)
+
+        lax.fori_loop(1, n_rows, drain, 0)
+
+        def drain_v(k, carry):
+            v_copy(k, ((chip + k) % chips) * 2 + core, r).wait_send()
+            return carry
+
+        lax.fori_loop(1, chips, drain_v, 0)
+        own.wait_send()
+
+        def drain_f(k, carry):
+            f_copy(k, ((chip + chips - k) % chips) * 2 + core).wait_send()
+            return carry
+
+        lax.fori_loop(1, chips, drain_f, 0)
+
 
     node_hist(acc_ref, parent_ref, small_ref, evict_ref, hist_ref, nodes)
     partial = gain_terms(hist_ref, nodes)

time: 96.8 us -> 76.9 us (0.79); the launches traced: 95.4 us -> 76.6 us
  Pallas kernels: 85.1 us -> 66.3 us
    pallas_call x1, Pallas kernels: 85.1 us -> 66.3 us  [gather_hist(): pl.pallas_call(functools.partial(gather_hist_kernel, nodes=nodes, targets...]
where the time goes in v10:
time: 76.9 us; the launch traced here: 76.6 us
  Pallas kernels  66.3 us (86%)
  local copies, waits for them, and re-layouts  6.62 us (9%)
  other arithmetic  3.02 us (4%)
    pallas_call x1, Pallas kernels, gather_hist(): pl.pallas_call(functools.partial(gather_hist_kernel, nodes=nodes, targets...  66.3 us
    unnamed x6, local copies, waits for them, and re-layouts  3.2 us
    convert_element_type x1, other arithmetic, local(): seg = (node_of_row[:, None] * BINS + codes).astype(jnp.int16)  1.67 us

profile of v10, /device:TPU:1, one launch (start us, length us, event | category | flops | bytes accessed | tf_op | source)
XLA Modules:
  0.0 76.6 jit_solution(9561648661377777014)
XLA Ops:
  0.6 0.7 broadcast_multiply_fusion
  1.3 1.7 %add_convert_fusion = s16[1536,256]{1,0:T(8,128)(2,1)S(1)} fusion(s32[1536,256]{1,0:T(8,128)} %param.7, s32[1536]{0:T(1024)S(1)} %broadcast_multiply_fusion), kind=kLoop, calls=%fused_computation | loop fusion | flops 786432 | bytes 2365440 | tf_op jit(solution)/shard_map/convert_element_type | solution.py:434
  3.0 0.7 copy.11
  3.7 0.0 copy-start
  3.7 0.0 copy-start.1
  3.7 0.2 reshape.20
  3.9 1.2 %reshape.21.seg_ref = s16[32,16,768]{2,1,0:T(8,128)(2,1)} reshape(s16[32,8,2,768]{3,2,1,0:T(2,128)(2,1)S(1)} %bitcast.7) | data formatting | bytes 1572864 | tf_op jit(solution)/shard_map/reshape | solution.py:435
  5.1 0.0 copy-done
  5.1 0.0 copy-done.1
  5.1 0.6 pad_maximum_fusion.v_ref
  5.8 66.3 %shard_map.94 = (f32[512,256]{1,0:T(8,128)}, f32[16,256]{1,0:T(8,128)}, f32[16,128]{1,0:T(8,128)}) custom-call(s32[8]{0:T(128)} %small_ref.1, s32[8]{0:T(128)} %evict_ref.1, s16[32,16,768]{2,1,0:T(8,128)(2,1)} %reshape.21.seg_ref, bf16[32,1536]{1,0:T(8,128)(2,1)} %pad_maximum_fusion.v_ref, f32[256,256]{1,0:T(8,128)} %bitcast.11), custom_call_target="tpu_custom_call" | custom-call | flops 12884901888 | bytes 4456448 | tf_op jit(solution)/shard_map/pallas_call | solution.py:391
  72.1 1.3 %slice_reduce_fusion = f32[16]{0:T(128)} fusion(f32[16,128]{1,0:T(8,128)} %get-tuple-element.8), kind=kLoop, calls=%fused_computation.2 | loop fusion | bytes 128 | tf_op jit(solution)/shard_map/slice | solution.py:441
  73.4 1.9 %copy.14 = f32[2,16,16,256]{3,2,1,0:T(8,128)} copy(f32[2,16,16,256]{3,2,1,0:T(8,128)} %bitcast.8) | data formatting | bytes 1048576
  75.3 1.3 %copy.15 = f32[16,256]{1,0:T(8,128)} copy(f32[16,256]{1,0:T(8,128)} %get-tuple-element.13) | data formatting | bytes 32768
Async XLA Ops:
  3.7 1.5 %copy-start = (bf16[1536,16]{0,1:T(8,128)(2,1)S(1)}, bf16[1536,16]{0,1:T(8,128)(2,1)}, u32[]{:S(2)}) copy-start(bf16[1536,16]{0,1:T(8,128)(2,1)} %param.10) | copy-start | bytes 147460
  3.7 1.4 %copy-start.1 = (bf16[1536,16]{0,1:T(8,128)(2,1)S(1)}, bf16[1536,16]{0,1:T(8,128)(2,1)}, u32[]{:S(2)}) copy-start(bf16[1536,16]{0,1:T(8,128)(2,1)} %param.9) | copy-start | bytes 147460

commit v11 on v10

--- a/solution.py
+++ b/solution.py
@@ -181,7 +181,7 @@
             slot = dev((i * 3) % 4, db)
             arrive(slot)
             if relay:
-                copy(vbuf.at[slot], vsend.at[11 + i], dev(0, 1), slot).start()
+                copy(vbuf.at[slot], vsend.at[11 + i], dev(0, -db), slot).start()
             copy(vbuf.at[slot], fsend.at[first + i], partner, slot).start()
             compute(slot)
             return carry
@@ -192,15 +192,15 @@
         def body(i, carry):
             slot = dev((i * 3) % 4, db)
             if relay:
-                copy(vbuf.at[slot], vsend.at[11 + i], dev(0, 1), slot).wait_send()
+                copy(vbuf.at[slot], vsend.at[11 + i], dev(0, -db), slot).wait_send()
             copy(vbuf.at[slot], fsend.at[first + i], partner, slot).wait_send()
             return carry
 
         return body
 
-    rows_plan = [(-1, True, 4), (1, False, 8), (-2, False, 12)]
-    for db, relay, first in rows_plan:
-        lax.fori_loop(0, 4, row_step(db, relay, first), 0)
+    rows_plan = [(-1, True, 4, 0, 2), (1, False, 8, 0, 2), (-1, False, 4, 2, 4), (1, True, 8, 2, 4), (2, False, 12, 0, 4)]
+    for db, relay, first, lo, hi in rows_plan:
+        lax.fori_loop(lo, hi, row_step(db, relay, first), 0)
 
     def take_partner(k, carry):
         slot = ((chip + 16 - k) % 16) * 2 + 1 - core
@@ -211,8 +211,8 @@
     lax.fori_loop(0, 16, take_partner, 0)
     for c in started:
         c.wait_send()
-    for db, relay, first in rows_plan:
-        lax.fori_loop(0, 4, row_drain(db, relay, first), 0)
+    for db, relay, first, lo, hi in rows_plan:
+        lax.fori_loop(lo, hi, row_drain(db, relay, first), 0)
 
 
 def gather_hist_kernel(

time: 76.9 us -> 77.6 us (level)
  no operation moved by 1% of the time
where the time goes in v11:
time: 77.6 us; the launch traced here: 77.3 us
  Pallas kernels  67 us (86%)
  local copies, waits for them, and re-layouts  6.62 us (9%)
  other arithmetic  3.02 us (4%)
    pallas_call x1, Pallas kernels, gather_hist(): pl.pallas_call(functools.partial(gather_hist_kernel, nodes=nodes, targets...  67 us
    unnamed x6, local copies, waits for them, and re-layouts  3.2 us
    convert_element_type x1, other arithmetic, local(): seg = (node_of_row[:, None] * BINS + codes).astype(jnp.int16)  1.67 us

profile of v11, /device:TPU:1, one launch (start us, length us, event | category | flops | bytes accessed | tf_op | source)
XLA Modules:
  0.0 77.3 jit_solution(17029562187543420529)
XLA Ops:
  0.6 0.7 broadcast_multiply_fusion
  1.3 1.7 %add_convert_fusion = s16[1536,256]{1,0:T(8,128)(2,1)S(1)} fusion(s32[1536,256]{1,0:T(8,128)} %param.7, s32[1536]{0:T(1024)S(1)} %broadcast_multiply_fusion), kind=kLoop, calls=%fused_computation | loop fusion | flops 786432 | bytes 2365440 | tf_op jit(solution)/shard_map/convert_element_type | solution.py:434
  3.0 0.7 copy.11
  3.7 0.0 copy-start
  3.7 0.0 copy-start.1
  3.7 0.2 reshape.20
  3.9 1.2 %reshape.21.seg_ref = s16[32,16,768]{2,1,0:T(8,128)(2,1)} reshape(s16[32,8,2,768]{3,2,1,0:T(2,128)(2,1)S(1)} %bitcast.7) | data formatting | bytes 1572864 | tf_op jit(solution)/shard_map/reshape | solution.py:435
  5.1 0.0 copy-done
  5.1 0.0 copy-done.1
  5.1 0.6 pad_maximum_fusion.v_ref
  5.8 67.0 %shard_map.94 = (f32[512,256]{1,0:T(8,128)}, f32[16,256]{1,0:T(8,128)}, f32[16,128]{1,0:T(8,128)}) custom-call(s32[8]{0:T(128)} %small_ref.1, s32[8]{0:T(128)} %evict_ref.1, s16[32,16,768]{2,1,0:T(8,128)(2,1)} %reshape.21.seg_ref, bf16[32,1536]{1,0:T(8,128)(2,1)} %pad_maximum_fusion.v_ref, f32[256,256]{1,0:T(8,128)} %bitcast.11), custom_call_target="tpu_custom_call" | custom-call | flops 12884901888 | bytes 4456448 | tf_op jit(solution)/shard_map/pallas_call | solution.py:391
  72.8 1.3 %slice_reduce_fusion = f32[16]{0:T(128)} fusion(f32[16,128]{1,0:T(8,128)} %get-tuple-element.8), kind=kLoop, calls=%fused_computation.2 | loop fusion | bytes 128 | tf_op jit(solution)/shard_map/slice | solution.py:441
  74.1 1.9 %copy.14 = f32[2,16,16,256]{3,2,1,0:T(8,128)} copy(f32[2,16,16,256]{3,2,1,0:T(8,128)} %bitcast.8) | data formatting | bytes 1048576
  76.0 1.3 %copy.15 = f32[16,256]{1,0:T(8,128)} copy(f32[16,256]{1,0:T(8,128)} %get-tuple-element.13) | data formatting | bytes 32768
Async XLA Ops:
  3.7 1.5 %copy-start = (bf16[1536,16]{0,1:T(8,128)(2,1)S(1)}, bf16[1536,16]{0,1:T(8,128)(2,1)}, u32[]{:S(2)}) copy-start(bf16[1536,16]{0,1:T(8,128)(2,1)} %param.10) | copy-start | bytes 147460
  3.7 1.4 %copy-start.1 = (bf16[1536,16]{0,1:T(8,128)(2,1)S(1)}, bf16[1536,16]{0,1:T(8,128)(2,1)}, u32[]{:S(2)}) copy-start(bf16[1536,16]{0,1:T(8,128)(2,1)} %param.9) | copy-start | bytes 147460

commit v12 on v11

--- a/solution.py
+++ b/solution.py
@@ -422,6 +422,183 @@
     )(small_side, evicted, seg_p, v_loc, parent)
 
 
+def pair_split_kernel(
+    small_ref, evict_ref, seg_ref, v_ref, parent_ref, hist_ref, split_ref, best_ref,
+    acc_ref, vbuf, sbuf, pbuf, vsend, vrecv, ssend, srecv, psend, precv, gbuf, mbuf, gsend, grecv, msend, mrecv,
+    *, nodes, targets,
+):
+    n_rows = lax.axis_size("rows")
+    n_outs = lax.axis_size("outs")
+    r = lax.axis_index("rows")
+    o = lax.axis_index("outs")
+    core = r % 2
+    chip = r // 2
+    y = chip // 4
+    x = chip % 4
+    a = x + core * (y - x)
+    b = y + core * (x - y)
+    partner = chip * 2 + 1 - core
+    barrier = pltpu.get_barrier_semaphore()
+
+    def greet(k, carry):
+        pl.semaphore_signal(barrier, 1, device_id=((r + k) % n_rows, o), device_id_type=MESH_ID)
+        return carry
+
+    lax.fori_loop(1, n_rows, greet, 0)
+    for k in range(1, n_outs):
+        pl.semaphore_signal(barrier, 1, device_id=(r, (o + k) % n_outs), device_id_type=MESH_ID)
+    acc_ref[...] = jnp.zeros_like(acc_ref)
+    block_hist(acc_ref, v_ref[...], seg_ref[chip].astype(jnp.int32), nodes)
+    pl.semaphore_wait(barrier, n_rows - 1 + n_outs - 1)
+
+    def dev(da, db):
+        ap = (a + da + 4) % 4
+        bp = (b + db + 4) % 4
+        return ((1 - core) * (bp * 4 + ap) + core * (ap * 4 + bp)) * 2 + core
+
+    def copy(src, sem, peer, slot):
+        return pltpu.make_async_remote_copy(
+            src_ref=src, dst_ref=vbuf.at[slot], send_sem=sem, recv_sem=vrecv.at[slot],
+            device_id=(peer, o), device_id_type=MESH_ID,
+        )
+
+    def s_copy(k, peer, slot):
+        return pltpu.make_async_remote_copy(
+            src_ref=seg_ref.at[peer // 2], dst_ref=sbuf.at[slot], send_sem=ssend.at[k], recv_sem=srecv.at[slot],
+            device_id=(peer, o), device_id_type=MESH_ID,
+        )
+
+    def seg_peer(k):
+        return ((chip + k) % 16) * 2 + core
+
+    def arrive(slot):
+        copy(vbuf.at[slot], vsend.at[0], partner, slot).wait_recv()
+        s_copy(0, slot, slot).wait_recv()
+
+    def compute(slot):
+        block_hist(acc_ref, vbuf[slot], sbuf[slot].astype(jnp.int32), nodes)
+
+    started = []
+
+    def start(src, sem, peer, slot):
+        c = copy(src, sem, peer, slot)
+        c.start()
+        started.append(c)
+
+    for j, (da, db) in enumerate([(1, 0), (-1, 0), (0, 1), (0, -1)]):
+        start(v_ref, vsend.at[j], dev(da, db), r)
+
+    def send_seg(k, carry):
+        s_copy(k, seg_peer(k), r).start()
+        return carry
+
+    lax.fori_loop(1, 16, send_seg, 0)
+
+    sem = 4
+    for da in [-1, 1, -2]:
+        slot = dev(da, 0)
+        arrive(slot)
+        if da == -1:
+            start(vbuf.at[slot], vsend.at[sem], dev(1, 0), slot)
+            sem += 1
+        start(vbuf.at[slot], vsend.at[sem], dev(0, 1), slot)
+        start(vbuf.at[slot], vsend.at[sem + 1], dev(0, -1), slot)
+        sem += 2
+        compute(slot)
+
+    def row_step(db, relay):
+        def body(i, carry):
+            slot = dev((i * 3) % 4, db)
+            arrive(slot)
+            if relay:
+                copy(vbuf.at[slot], vsend.at[11 + i], dev(0, 1), slot).start()
+            compute(slot)
+            return carry
+
+        return body
+
+    for db, relay in [(-1, True), (1, False), (-2, False)]:
+        lax.fori_loop(0, 4, row_step(db, relay), 0)
+
+    span = hist_ref.shape[1]
+    mine = pl.ds(pl.multiple_of(core * span, span), span)
+    theirs = pl.ds(pl.multiple_of((1 - core) * span, span), span)
+    swap = pltpu.make_async_remote_copy(
+        src_ref=acc_ref.at[:, theirs], dst_ref=pbuf, send_sem=psend, recv_sem=precv,
+        device_id=(partner, o), device_id_type=MESH_ID,
+    )
+    swap.start()
+    swap.wait_recv()
+    hist_ref[...] = acc_ref[:, mine] + pbuf[...]
+    swap.wait_send()
+    for c in started:
+        c.wait_send()
+
+    def relay_drain(i, carry):
+        slot = dev((i * 3) % 4, -1)
+        copy(vbuf.at[slot], vsend.at[11 + i], dev(0, 1), slot).wait_send()
+        return carry
+
+    lax.fori_loop(0, 4, relay_drain, 0)
+
+    def drain(k, carry):
+        s_copy(k, seg_peer(k), r).wait_send()
+        return carry
+
+    lax.fori_loop(1, 16, drain, 0)
+
+    node_hist(hist_ref, parent_ref, small_ref, evict_ref, hist_ref, nodes)
+    partial = gain_terms(hist_ref, nodes)
+    exchange(partial, split_ref, best_ref, gbuf, mbuf, gsend, grecv, msend, mrecv, targets)
+
+
+def pair_split(small_side, evicted, seg_c, v_loc, parent, nodes, targets):
+    chips, width, half = seg_c.shape
+    n_rows = 2 * chips
+    n_outs = lax.axis_size("outs")
+    vw, rows = v_loc.shape
+    cols = width // 2 * BINS
+    span = cols // 2
+    out_rows = vw * nodes
+    total = n_rows * rows
+    vmem = pl.BlockSpec(memory_space=pltpu.VMEM)
+    smem = pl.BlockSpec(memory_space=pltpu.SMEM)
+    return pl.pallas_call(
+        functools.partial(pair_split_kernel, nodes=nodes, targets=targets),
+        out_shape=(
+            jax.ShapeDtypeStruct((out_rows, span), jnp.float32),
+            jax.ShapeDtypeStruct((nodes, span), jnp.float32),
+            jax.ShapeDtypeStruct((nodes, 128), jnp.float32),
+        ),
+        in_specs=[smem, smem, vmem, vmem, vmem],
+        out_specs=(vmem, vmem, vmem),
+        scratch_shapes=[
+            pltpu.VMEM((out_rows, cols), jnp.float32),
+            pltpu.VMEM((n_rows, vw, rows), v_loc.dtype),
+            pltpu.VMEM((n_rows, width, half), seg_c.dtype),
+            pltpu.VMEM((out_rows, span), jnp.float32),
+            pltpu.SemaphoreType.DMA((chips,)),
+            pltpu.SemaphoreType.DMA((n_rows,)),
+            pltpu.SemaphoreType.DMA((chips,)),
+            pltpu.SemaphoreType.DMA((n_rows,)),
+            pltpu.SemaphoreType.DMA(()),
+            pltpu.SemaphoreType.DMA(()),
+            pltpu.VMEM((n_outs, nodes, span), jnp.float32),
+            pltpu.VMEM((n_rows, nodes, 128), jnp.float32),
+            pltpu.SemaphoreType.DMA((n_outs,)),
+            pltpu.SemaphoreType.DMA((n_outs,)),
+            pltpu.SemaphoreType.DMA((n_rows,)),
+            pltpu.SemaphoreType.DMA((n_rows,)),
+        ],
+        compiler_params=pltpu.CompilerParams(collective_id=2, has_side_effects=True),
+        cost_estimate=pl.CostEstimate(
+            flops=2 * out_rows * cols * total // 2,
+            bytes_accessed=total * (vw * 2 + width) + out_rows * cols * 4,
+            transcendentals=0,
+        ),
+    )(small_side, evicted, seg_c, v_loc, parent)
+
+
 def local(codes, node_of_row, grad, hess, small_side, evicted, parent_hist):
     pairs = small_side.shape[0]
     nodes = 2 * pairs
@@ -436,7 +613,13 @@
     v_loc = jnp.concatenate([grad.T, hess.T], axis=0)
     span = feats * BINS
     parent = parent_hist.reshape(2 * pairs * local_targets, span)
-    hist, split_gain, best = gather_hist(small_side, evicted, seg_p, v_loc, parent, nodes, targets)
+    if n_rows == 32:
+        seg_c = jnp.transpose(seg.reshape(2, half, n_rows // 2, 2 * feats), (2, 3, 0, 1)).reshape(
+            n_rows // 2, 4 * feats, half
+        )
+        hist, split_gain, best = pair_split(small_side, evicted, seg_c, v_loc, parent, nodes, targets)
+    else:
+        hist, split_gain, best = gather_hist(small_side, evicted, seg_p, v_loc, parent, nodes, targets)
     node_hist = hist.reshape(2, nodes, local_targets, span)
     return (node_hist, split_gain, best[:, 0])
 

time: 77.6 us -> 73.5 us (0.947)
  Pallas kernels: 67 us -> 62.9 us
    pallas_call x1, Pallas kernels: 67 us -> 62.9 us  [pair_split(): pl.pallas_call(functools.partial(pair_split_kernel, nodes=nodes, targets=...]
where the time goes in v12:
time: 73.5 us; the launch traced here: 73.2 us
  Pallas kernels  62.9 us (86%)
  local copies, waits for them, and re-layouts  6.62 us (9%)
  other arithmetic  3.02 us (4%)
    pallas_call x1, Pallas kernels, pair_split(): pl.pallas_call(functools.partial(pair_split_kernel, nodes=nodes, targets=...  62.9 us
    unnamed x6, local copies, waits for them, and re-layouts  3.2 us
    convert_element_type x1, other arithmetic, local(): seg = (node_of_row[:, None] * BINS + codes).astype(jnp.int16)  1.67 us

profile of v12, /device:TPU:1, one launch (start us, length us, event | category | flops | bytes accessed | tf_op | source)
XLA Modules:
  0.0 73.2 jit_solution(11137921719420678140)
XLA Ops:
  0.6 0.7 broadcast_multiply_fusion
  1.3 1.7 %add_convert_fusion = s16[1536,256]{1,0:T(8,128)(2,1)S(1)} fusion(s32[1536,256]{1,0:T(8,128)} %param.7, s32[1536]{0:T(1024)S(1)} %broadcast_multiply_fusion), kind=kLoop, calls=%fused_computation | loop fusion | flops 786432 | bytes 2365440 | tf_op jit(solution)/shard_map/convert_element_type | solution.py:611
  3.0 0.7 copy.11
  3.7 0.0 copy-start
  3.7 0.0 copy-start.1
  3.7 0.2 reshape.20
  3.9 1.2 %reshape.21.seg_ref = s16[16,32,768]{2,1,0:T(8,128)(2,1)} reshape(s16[16,16,2,768]{3,2,1,0:T(2,128)(2,1)S(1)} %bitcast.7) | data formatting | bytes 1572864 | tf_op jit(solution)/shard_map/reshape | solution.py:617
  5.1 0.0 copy-done
  5.1 0.0 copy-done.1
  5.1 0.6 pad_maximum_fusion.v_ref
  5.8 62.9 %shard_map.94 = (f32[512,256]{1,0:T(8,128)}, f32[16,256]{1,0:T(8,128)}, f32[16,128]{1,0:T(8,128)}) custom-call(s32[8]{0:T(128)} %small_ref.1, s32[8]{0:T(128)} %evict_ref.1, s16[16,32,768]{2,1,0:T(8,128)(2,1)} %reshape.21.seg_ref, bf16[32,1536]{1,0:T(8,128)(2,1)} %pad_maximum_fusion.v_ref, f32[256,256]{1,0:T(8,128)} %bitcast.11), custom_call_target="tpu_custom_call" | custom-call | flops 12884901888 | bytes 5767168 | tf_op jit(solution)/shard_map/pallas_call | solution.py:566
  68.7 1.3 %slice_reduce_fusion = f32[16]{0:T(128)} fusion(f32[16,128]{1,0:T(8,128)} %get-tuple-element.8), kind=kLoop, calls=%fused_computation.2 | loop fusion | bytes 128 | tf_op jit(solution)/shard_map/slice | solution.py:624
  70.0 1.9 %copy.14 = f32[2,16,16,256]{3,2,1,0:T(8,128)} copy(f32[2,16,16,256]{3,2,1,0:T(8,128)} %bitcast.8) | data formatting | bytes 1048576
  71.9 1.3 %copy.15 = f32[16,256]{1,0:T(8,128)} copy(f32[16,256]{1,0:T(8,128)} %get-tuple-element.13) | data formatting | bytes 32768
Async XLA Ops:
  3.7 1.5 %copy-start = (bf16[1536,16]{0,1:T(8,128)(2,1)S(1)}, bf16[1536,16]{0,1:T(8,128)(2,1)}, u32[]{:S(2)}) copy-start(bf16[1536,16]{0,1:T(8,128)(2,1)} %param.10) | copy-start | bytes 147460
  3.7 1.4 %copy-start.1 = (bf16[1536,16]{0,1:T(8,128)(2,1)S(1)}, bf16[1536,16]{0,1:T(8,128)(2,1)}, u32[]{:S(2)}) copy-start(bf16[1536,16]{0,1:T(8,128)(2,1)} %param.9) | copy-start | bytes 147460

commit v13 on v12

--- a/solution.py
+++ b/solution.py
@@ -614,9 +614,8 @@
     span = feats * BINS
     parent = parent_hist.reshape(2 * pairs * local_targets, span)
     if n_rows == 32:
-        seg_c = jnp.transpose(seg.reshape(2, half, n_rows // 2, 2 * feats), (2, 3, 0, 1)).reshape(
-            n_rows // 2, 4 * feats, half
-        )
+        seg_t = (codes.T + node_of_row[None, :] * BINS).astype(jnp.int16)
+        seg_c = seg_t.reshape(n_rows // 2, 2 * feats, 2, half).reshape(n_rows // 2, 4 * feats, half)
         hist, split_gain, best = pair_split(small_side, evicted, seg_c, v_loc, parent, nodes, targets)
     else:
         hist, split_gain, best = gather_hist(small_side, evicted, seg_p, v_loc, parent, nodes, targets)

time: 73.5 us -> 73.2 us (level)
    reshape x2 -> x0, local copies, waits for them, and re-layouts: 1.42 us -> none  [the longest x1 1.21 us: local(): jnp.transpose(seg.reshape(2, half, n_rows // 2, 2 * feats), (2, 3, 0, 1))]
    another operation x0 -> x1, local copies, waits for them, and re-layouts: none -> 1.15 us  [local(): seg_t.reshape(n_rows // 2, 2 * feats, 2, half)]
where the time goes in v13:
time: 73.2 us; the launch traced here: 72.9 us
  Pallas kernels  62.9 us (86%)
  local copies, waits for them, and re-layouts  6.34 us (9%)
  other arithmetic  3.02 us (4%)
    pallas_call x1, Pallas kernels, pair_split(): pl.pallas_call(functools.partial(pair_split_kernel, nodes=nodes, targets=...  62.9 us
    unnamed x6, local copies, waits for them, and re-layouts  3.2 us
    convert_element_type x1, other arithmetic, local(): seg_t = (codes.T + node_of_row[None, :] * BINS).astype(jnp.int16)  1.67 us

profile of v13, /device:TPU:1, one launch (start us, length us, event | category | flops | bytes accessed | tf_op | source)
XLA Modules:
  0.0 72.9 jit_solution(11237020349971755209)
XLA Ops:
  0.6 0.7 broadcast_multiply_fusion
  1.3 1.7 %fusion = s16[256,1536]{0,1:T(8,128)(2,1)S(1)} fusion(s32[1536,256]{1,0:T(8,128)} %param.7, s32[1536]{0:T(1024)S(1)} %broadcast_multiply_fusion), kind=kLoop, calls=%fused_computation.1 | loop fusion | flops 786432 | bytes 2365440 | tf_op jit(solution)/shard_map/convert_element_type | solution.py:617
  3.0 0.0 copy-start
  3.0 0.0 copy-start.1
  3.0 0.7 copy.11
  3.7 1.1 %reshape_reshape.3.seg_ref = s16[16,32,768]{2,1,0:T(8,128)(2,1)} reshape(s16[256,1536]{1,0:T(8,128)(2,1)S(1)} %copy.11) | data formatting | bytes 1572864 | tf_op jit(solution)/shard_map/reshape;reshape | solution.py:618
  4.9 0.0 copy-done
  4.9 0.0 copy-done.1
  4.9 0.6 pad_maximum_fusion.v_ref
  5.5 62.9 %shard_map.94 = (f32[512,256]{1,0:T(8,128)}, f32[16,256]{1,0:T(8,128)}, f32[16,128]{1,0:T(8,128)}) custom-call(s32[8]{0:T(128)} %small_ref.1, s32[8]{0:T(128)} %evict_ref.1, s16[16,32,768]{2,1,0:T(8,128)(2,1)} %reshape_reshape.3.seg_ref, bf16[32,1536]{1,0:T(8,128)(2,1)} %pad_maximum_fusion.v_ref, f32[256,256]{1,0:T(8,128)} %bitcast.9), custom_call_target="tpu_custom_call" | custom-call | flops 12884901888 | bytes 5767168 | tf_op jit(solution)/shard_map/pallas_call | solution.py:566
  68.4 1.3 %slice_reduce_fusion = f32[16]{0:T(128)} fusion(f32[16,128]{1,0:T(8,128)} %get-tuple-element.8), kind=kLoop, calls=%fused_computation.3 | loop fusion | bytes 128 | tf_op jit(solution)/shard_map/slice | solution.py:623
  69.7 1.9 %copy.14 = f32[2,16,16,256]{3,2,1,0:T(8,128)} copy(f32[2,16,16,256]{3,2,1,0:T(8,128)} %bitcast.6) | data formatting | bytes 1048576
  71.6 1.3 %copy.15 = f32[16,256]{1,0:T(8,128)} copy(f32[16,256]{1,0:T(8,128)} %get-tuple-element.13) | data formatting | bytes 32768
Async XLA Ops:
  3.0 1.8 %copy-start = (bf16[1536,16]{0,1:T(8,128)(2,1)S(1)}, bf16[1536,16]{0,1:T(8,128)(2,1)}, u32[]{:S(2)}) copy-start(bf16[1536,16]{0,1:T(8,128)(2,1)} %param.10) | copy-start | bytes 147460
  3.0 1.8 %copy-start.1 = (bf16[1536,16]{0,1:T(8,128)(2,1)S(1)}, bf16[1536,16]{0,1:T(8,128)(2,1)}, u32[]{:S(2)}) copy-start(bf16[1536,16]{0,1:T(8,128)(2,1)} %param.9) | copy-start | bytes 147460

commit v14 on v13

--- a/solution.py
+++ b/solution.py
@@ -34,34 +34,36 @@
     return [peer for stage in row_stages(r, n_rows) for peer in stage]
 
 
-def exchange(partial, split_ref, best_ref, gbuf, mbuf, gsend, grecv, msend, mrecv, targets):
+def exchange(part_fn, split_ref, best_ref, gbuf, mbuf, gsend, grecv, msend, mrecv, targets):
     n_rows = lax.axis_size("rows")
     n_outs = lax.axis_size("outs")
     r = lax.axis_index("rows")
     o = lax.axis_index("outs")
-    gbuf[o] = partial
+    nodes = gbuf.shape[1]
+    halves = [(0, nodes // 2), (nodes // 2, nodes)]
+
+    def part_copy(h, k, dst, slot):
+        lo, hi = halves[h]
+        return pltpu.make_async_remote_copy(
+            src_ref=gbuf.at[o, pl.ds(lo, hi - lo)],
+            dst_ref=gbuf.at[slot, pl.ds(lo, hi - lo)],
+            send_sem=gsend.at[h, k],
+            recv_sem=grecv.at[h, slot],
+            device_id=(r, dst),
+            device_id_type=MESH_ID,
+        )
+
     sends = []
-    for k in range(1, n_outs):
-        copy = pltpu.make_async_remote_copy(
-            src_ref=gbuf.at[o],
-            dst_ref=gbuf.at[o],
-            send_sem=gsend.at[k],
-            recv_sem=grecv.at[o],
-            device_id=(r, (o + k) % n_outs),
-            device_id_type=MESH_ID,
-        )
-        copy.start()
-        sends.append(copy)
-    for k in range(1, n_outs):
-        src = (o + n_outs - k) % n_outs
-        pltpu.make_async_remote_copy(
-            src_ref=gbuf.at[o],
-            dst_ref=gbuf.at[src],
-            send_sem=gsend.at[k],
-            recv_sem=grecv.at[src],
-            device_id=(r, src),
-            device_id_type=MESH_ID,
-        ).wait_recv()
+    for h, (lo, hi) in enumerate(halves):
+        gbuf[o, lo:hi] = part_fn(lo, hi)
+        for k in range(1, n_outs):
+            copy = part_copy(h, k, (o + k) % n_outs, o)
+            copy.start()
+            sends.append(copy)
+    for h in range(2):
+        for k in range(1, n_outs):
+            src = (o + n_outs - k) % n_outs
+            part_copy(h, k, src, src).wait_recv()
     for copy in sends:
         copy.wait_send()
     acc = gbuf[0]
@@ -321,8 +323,7 @@
 
 
     node_hist(acc_ref, parent_ref, small_ref, evict_ref, hist_ref, nodes)
-    partial = gain_terms(hist_ref, nodes)
-    exchange(partial, split_ref, best_ref, gbuf, mbuf, gsend, grecv, msend, mrecv, targets)
+    exchange(functools.partial(gain_terms, hist_ref, nodes), split_ref, best_ref, gbuf, mbuf, gsend, grecv, msend, mrecv, targets)
 
 
 def node_hist(acc_ref, parent_ref, small_ref, evict_ref, hist_ref, nodes):
@@ -359,13 +360,14 @@
     return x
 
 
-def gain_terms(hist_ref, nodes):
+def gain_terms(hist_ref, nodes, lo, hi):
     rows, span = hist_ref.shape
     half = rows // 2
     tl = half // nodes
-    lane = lax.broadcasted_iota(jnp.int32, (half, span), 1) % BINS
-    left_g = group_scan(hist_ref[0:half], False)
-    left_h = group_scan(hist_ref[half:rows], False)
+    count = (hi - lo) * tl
+    lane = lax.broadcasted_iota(jnp.int32, (count, span), 1) % BINS
+    left_g = group_scan(hist_ref[lo * tl : hi * tl], False)
+    left_h = group_scan(hist_ref[half + lo * tl : half + hi * tl], False)
     total_g = group_scan(jnp.where(lane == BINS - 1, left_g, 0.0), True)
     total_h = group_scan(jnp.where(lane == BINS - 1, left_h, 0.0), True)
 
@@ -375,7 +377,7 @@
     gain = (
         score(left_g, left_h) + score(total_g - left_g, total_h - left_h) - score(total_g, total_h)
     )
-    return jnp.sum(gain.reshape(nodes, tl, span), axis=1)
+    return jnp.sum(gain.reshape(hi - lo, tl, span), axis=1)
 
 
 def gather_hist(small_side, evicted, seg_p, v_loc, parent, nodes, targets):
@@ -408,8 +410,8 @@
             pltpu.SemaphoreType.DMA((n_rows,)),
             pltpu.VMEM((n_outs, nodes, cols), jnp.float32),
             pltpu.VMEM((n_rows, nodes, 128), jnp.float32),
-            pltpu.SemaphoreType.DMA((n_outs,)),
-            pltpu.SemaphoreType.DMA((n_outs,)),
+            pltpu.SemaphoreType.DMA((2, n_outs)),
+            pltpu.SemaphoreType.DMA((2, n_outs)),
             pltpu.SemaphoreType.DMA((n_rows,)),
             pltpu.SemaphoreType.DMA((n_rows,)),
         ],
@@ -548,8 +550,7 @@
     lax.fori_loop(1, 16, drain, 0)
 
     node_hist(hist_ref, parent_ref, small_ref, evict_ref, hist_ref, nodes)
-    partial = gain_terms(hist_ref, nodes)
-    exchange(partial, split_ref, best_ref, gbuf, mbuf, gsend, grecv, msend, mrecv, targets)
+    exchange(functools.partial(gain_terms, hist_ref, nodes), split_ref, best_ref, gbuf, mbuf, gsend, grecv, msend, mrecv, targets)
 
 
 def pair_split(small_side, evicted, seg_c, v_loc, parent, nodes, targets):
@@ -585,8 +586,8 @@
             pltpu.SemaphoreType.DMA(()),
             pltpu.VMEM((n_outs, nodes, span), jnp.float32),
             pltpu.VMEM((n_rows, nodes, 128), jnp.float32),
-            pltpu.SemaphoreType.DMA((n_outs,)),
-            pltpu.SemaphoreType.DMA((n_outs,)),
+            pltpu.SemaphoreType.DMA((2, n_outs)),
+            pltpu.SemaphoreType.DMA((2, n_outs)),
             pltpu.SemaphoreType.DMA((n_rows,)),
             pltpu.SemaphoreType.DMA((n_rows,)),
         ],

time: 73.2 us -> 72.6 us (level)
  no operation moved by 1% of the time
where the time goes in v14:
time: 72.6 us; the launch traced here: 72.3 us
  Pallas kernels  62.3 us (86%)
  local copies, waits for them, and re-layouts  6.34 us (9%)
  other arithmetic  3.02 us (4%)
    pallas_call x1, Pallas kernels, pair_split(): pl.pallas_call(functools.partial(pair_split_kernel, nodes=nodes, targets=...  62.3 us
    unnamed x6, local copies, waits for them, and re-layouts  3.2 us
    convert_element_type x1, other arithmetic, local(): seg_t = (codes.T + node_of_row[None, :] * BINS).astype(jnp.int16)  1.67 us

profile of v14, /device:TPU:1, one launch (start us, length us, event | category | flops | bytes accessed | tf_op | source)
XLA Modules:
  0.0 72.3 jit_solution(16237653012032114175)
XLA Ops:
  0.6 0.7 broadcast_multiply_fusion
  1.3 1.7 %fusion = s16[256,1536]{0,1:T(8,128)(2,1)S(1)} fusion(s32[1536,256]{1,0:T(8,128)} %param.7, s32[1536]{0:T(1024)S(1)} %broadcast_multiply_fusion), kind=kLoop, calls=%fused_computation.1 | loop fusion | flops 786432 | bytes 2365440 | tf_op jit(solution)/shard_map/convert_element_type | solution.py:618
  3.0 0.0 copy-start
  3.0 0.0 copy-start.1
  3.0 0.7 copy.11
  3.7 1.1 %reshape_reshape.3.seg_ref = s16[16,32,768]{2,1,0:T(8,128)(2,1)} reshape(s16[256,1536]{1,0:T(8,128)(2,1)S(1)} %copy.11) | data formatting | bytes 1572864 | tf_op jit(solution)/shard_map/reshape;reshape | solution.py:619
  4.9 0.0 copy-done
  4.9 0.0 copy-done.1
  4.9 0.6 pad_maximum_fusion.v_ref
  5.5 62.3 %shard_map.94 = (f32[512,256]{1,0:T(8,128)}, f32[16,256]{1,0:T(8,128)}, f32[16,128]{1,0:T(8,128)}) custom-call(s32[8]{0:T(128)} %small_ref.1, s32[8]{0:T(128)} %evict_ref.1, s16[16,32,768]{2,1,0:T(8,128)(2,1)} %reshape_reshape.3.seg_ref, bf16[32,1536]{1,0:T(8,128)(2,1)} %pad_maximum_fusion.v_ref, f32[256,256]{1,0:T(8,128)} %bitcast.9), custom_call_target="tpu_custom_call" | custom-call | flops 12884901888 | bytes 5767168 | tf_op jit(solution)/shard_map/pallas_call | solution.py:567
  67.8 1.3 %slice_reduce_fusion = f32[16]{0:T(128)} fusion(f32[16,128]{1,0:T(8,128)} %get-tuple-element.8), kind=kLoop, calls=%fused_computation.3 | loop fusion | bytes 128 | tf_op jit(solution)/shard_map/slice | solution.py:624
  69.1 1.9 %copy.14 = f32[2,16,16,256]{3,2,1,0:T(8,128)} copy(f32[2,16,16,256]{3,2,1,0:T(8,128)} %bitcast.6) | data formatting | bytes 1048576
  71.0 1.3 %copy.15 = f32[16,256]{1,0:T(8,128)} copy(f32[16,256]{1,0:T(8,128)} %get-tuple-element.13) | data formatting | bytes 32768
Async XLA Ops:
  3.0 1.8 %copy-start = (bf16[1536,16]{0,1:T(8,128)(2,1)S(1)}, bf16[1536,16]{0,1:T(8,128)(2,1)}, u32[]{:S(2)}) copy-start(bf16[1536,16]{0,1:T(8,128)(2,1)} %param.10) | copy-start | bytes 147460
  3.0 1.8 %copy-start.1 = (bf16[1536,16]{0,1:T(8,128)(2,1)S(1)}, bf16[1536,16]{0,1:T(8,128)(2,1)}, u32[]{:S(2)}) copy-start(bf16[1536,16]{0,1:T(8,128)(2,1)} %param.9) | copy-start | bytes 147460

commit v15 on v14

--- a/solution.py
+++ b/solution.py
@@ -496,8 +496,23 @@
 
     lax.fori_loop(1, 16, send_seg, 0)
 
+    def row_step(db, relay):
+        def body(i, carry):
+            slot = dev((i * 3) % 4, db)
+            arrive(slot)
+            if relay:
+                copy(vbuf.at[slot], vsend.at[11 + i], dev(0, 1), slot).start()
+            compute(slot)
+            return carry
+
+        return body
+
     sem = 4
-    for da in [-1, 1, -2]:
+    for da in [-1, 1, None, -2]:
+        if da is None:
+            for db, relay in [(-1, True), (1, False)]:
+                lax.fori_loop(0, 1, row_step(db, relay), 0)
+            continue
         slot = dev(da, 0)
         arrive(slot)
         if da == -1:
@@ -507,20 +522,8 @@
         start(vbuf.at[slot], vsend.at[sem + 1], dev(0, -1), slot)
         sem += 2
         compute(slot)
-
-    def row_step(db, relay):
-        def body(i, carry):
-            slot = dev((i * 3) % 4, db)
-            arrive(slot)
-            if relay:
-                copy(vbuf.at[slot], vsend.at[11 + i], dev(0, 1), slot).start()
-            compute(slot)
-            return carry
-
-        return body
-
-    for db, relay in [(-1, True), (1, False), (-2, False)]:
-        lax.fori_loop(0, 4, row_step(db, relay), 0)
+    for db, relay, lo in [(-1, True, 1), (1, False, 1), (-2, False, 0)]:
+        lax.fori_loop(lo, 4, row_step(db, relay), 0)
 
     span = hist_ref.shape[1]
     mine = pl.ds(pl.multiple_of(core * span, span), span)

time: 72.6 us -> 71.4 us (0.983)
  Pallas kernels: 62.3 us -> 61.1 us
    pallas_call x1, Pallas kernels: 62.3 us -> 61.1 us  [pair_split(): pl.pallas_call(functools.partial(pair_split_kernel, nodes=nodes, targets=...]
where the time goes in v15:
time: 71.4 us; the launch traced here: 71.1 us
  Pallas kernels  61.1 us (86%)
  local copies, waits for them, and re-layouts  6.34 us (9%)
  other arithmetic  3.02 us (4%)
    pallas_call x1, Pallas kernels, pair_split(): pl.pallas_call(functools.partial(pair_split_kernel, nodes=nodes, targets=...  61.1 us
    unnamed x6, local copies, waits for them, and re-layouts  3.2 us
    convert_element_type x1, other arithmetic, local(): seg_t = (codes.T + node_of_row[None, :] * BINS).astype(jnp.int16)  1.67 us

profile of v15, /device:TPU:1, one launch (start us, length us, event | category | flops | bytes accessed | tf_op | source)
XLA Modules:
  0.0 71.1 jit_solution(13382682436874385662)
XLA Ops:
  0.6 0.7 broadcast_multiply_fusion
  1.3 1.7 %fusion = s16[256,1536]{0,1:T(8,128)(2,1)S(1)} fusion(s32[1536,256]{1,0:T(8,128)} %param.7, s32[1536]{0:T(1024)S(1)} %broadcast_multiply_fusion), kind=kLoop, calls=%fused_computation.1 | loop fusion | flops 786432 | bytes 2365440 | tf_op jit(solution)/shard_map/convert_element_type | solution.py:621
  3.0 0.0 copy-start
  3.0 0.0 copy-start.1
  3.0 0.7 copy.11
  3.7 1.1 %reshape_reshape.3.seg_ref = s16[16,32,768]{2,1,0:T(8,128)(2,1)} reshape(s16[256,1536]{1,0:T(8,128)(2,1)S(1)} %copy.11) | data formatting | bytes 1572864 | tf_op jit(solution)/shard_map/reshape;reshape | solution.py:622
  4.9 0.0 copy-done
  4.9 0.0 copy-done.1
  4.9 0.6 pad_maximum_fusion.v_ref
  5.5 61.1 %shard_map.94 = (f32[512,256]{1,0:T(8,128)}, f32[16,256]{1,0:T(8,128)}, f32[16,128]{1,0:T(8,128)}) custom-call(s32[8]{0:T(128)} %small_ref.1, s32[8]{0:T(128)} %evict_ref.1, s16[16,32,768]{2,1,0:T(8,128)(2,1)} %reshape_reshape.3.seg_ref, bf16[32,1536]{1,0:T(8,128)(2,1)} %pad_maximum_fusion.v_ref, f32[256,256]{1,0:T(8,128)} %bitcast.9), custom_call_target="tpu_custom_call" | custom-call | flops 12884901888 | bytes 5767168 | tf_op jit(solution)/shard_map/pallas_call | solution.py:570
  66.6 1.3 %slice_reduce_fusion = f32[16]{0:T(128)} fusion(f32[16,128]{1,0:T(8,128)} %get-tuple-element.8), kind=kLoop, calls=%fused_computation.3 | loop fusion | bytes 128 | tf_op jit(solution)/shard_map/slice | solution.py:627
  67.9 1.9 %copy.14 = f32[2,16,16,256]{3,2,1,0:T(8,128)} copy(f32[2,16,16,256]{3,2,1,0:T(8,128)} %bitcast.6) | data formatting | bytes 1048576
  69.8 1.3 %copy.15 = f32[16,256]{1,0:T(8,128)} copy(f32[16,256]{1,0:T(8,128)} %get-tuple-element.13) | data formatting | bytes 32768
Async XLA Ops:
  3.0 1.8 %copy-start = (bf16[1536,16]{0,1:T(8,128)(2,1)S(1)}, bf16[1536,16]{0,1:T(8,128)(2,1)}, u32[]{:S(2)}) copy-start(bf16[1536,16]{0,1:T(8,128)(2,1)} %param.10) | copy-start | bytes 147460
  3.0 1.8 %copy-start.1 = (bf16[1536,16]{0,1:T(8,128)(2,1)S(1)}, bf16[1536,16]{0,1:T(8,128)(2,1)}, u32[]{:S(2)}) copy-start(bf16[1536,16]{0,1:T(8,128)(2,1)} %param.9) | copy-start | bytes 147460

commit v16 on v15

--- a/solution.py
+++ b/solution.py
@@ -424,6 +424,10 @@
     )(small_side, evicted, seg_p, v_loc, parent)
 
 
+def forward_order(i):
+    return (3 * i + (i // 2) * (2 * i - 1)) % 4
+
+
 def pair_split_kernel(
     small_ref, evict_ref, seg_ref, v_ref, parent_ref, hist_ref, split_ref, best_ref,
     acc_ref, vbuf, sbuf, pbuf, vsend, vrecv, ssend, srecv, psend, precv, gbuf, mbuf, gsend, grecv, msend, mrecv,
@@ -498,7 +502,7 @@
 
     def row_step(db, relay):
         def body(i, carry):
-            slot = dev((i * 3) % 4, db)
+            slot = dev(forward_order(i), db)
             arrive(slot)
             if relay:
                 copy(vbuf.at[slot], vsend.at[11 + i], dev(0, 1), slot).start()
@@ -540,7 +544,7 @@
         c.wait_send()
 
     def relay_drain(i, carry):
-        slot = dev((i * 3) % 4, -1)
+        slot = dev(forward_order(i), -1)
         copy(vbuf.at[slot], vsend.at[11 + i], dev(0, 1), slot).wait_send()
         return carry
 

time: 71.4 us -> 70.6 us (0.989)
  Pallas kernels: 61.1 us -> 60.2 us
    pallas_call x1, Pallas kernels: 61.1 us -> 60.2 us  [pair_split(): pl.pallas_call(functools.partial(pair_split_kernel, nodes=nodes, targets=...]
where the time goes in v16:
time: 70.6 us; the launch traced here: 70.3 us
  Pallas kernels  60.2 us (85%)
  local copies, waits for them, and re-layouts  6.34 us (9%)
  other arithmetic  3.02 us (4%)
    pallas_call x1, Pallas kernels, pair_split(): pl.pallas_call(functools.partial(pair_split_kernel, nodes=nodes, targets=...  60.2 us
    unnamed x6, local copies, waits for them, and re-layouts  3.2 us
    convert_element_type x1, other arithmetic, local(): seg_t = (codes.T + node_of_row[None, :] * BINS).astype(jnp.int16)  1.67 us

profile of v16, /device:TPU:1, one launch (start us, length us, event | category | flops | bytes accessed | tf_op | source)
XLA Modules:
  0.0 70.3 jit_solution(8641814031420078824)
XLA Ops:
  0.6 0.7 broadcast_multiply_fusion
  1.3 1.7 %fusion = s16[256,1536]{0,1:T(8,128)(2,1)S(1)} fusion(s32[1536,256]{1,0:T(8,128)} %param.7, s32[1536]{0:T(1024)S(1)} %broadcast_multiply_fusion), kind=kLoop, calls=%fused_computation.1 | loop fusion | flops 786432 | bytes 2365440 | tf_op jit(solution)/shard_map/convert_element_type | solution.py:625
  3.0 0.0 copy-start
  3.0 0.0 copy-start.1
  3.0 0.7 copy.11
  3.7 1.1 %reshape_reshape.3.seg_ref = s16[16,32,768]{2,1,0:T(8,128)(2,1)} reshape(s16[256,1536]{1,0:T(8,128)(2,1)S(1)} %copy.11) | data formatting | bytes 1572864 | tf_op jit(solution)/shard_map/reshape;reshape | solution.py:626
  4.9 0.0 copy-done
  4.9 0.0 copy-done.1
  4.9 0.6 pad_maximum_fusion.v_ref
  5.5 60.2 %shard_map.94 = (f32[512,256]{1,0:T(8,128)}, f32[16,256]{1,0:T(8,128)}, f32[16,128]{1,0:T(8,128)}) custom-call(s32[8]{0:T(128)} %small_ref.1, s32[8]{0:T(128)} %evict_ref.1, s16[16,32,768]{2,1,0:T(8,128)(2,1)} %reshape_reshape.3.seg_ref, bf16[32,1536]{1,0:T(8,128)(2,1)} %pad_maximum_fusion.v_ref, f32[256,256]{1,0:T(8,128)} %bitcast.9), custom_call_target="tpu_custom_call" | custom-call | flops 12884901888 | bytes 5767168 | tf_op jit(solution)/shard_map/pallas_call | solution.py:574
  65.7 1.3 %slice_reduce_fusion = f32[16]{0:T(128)} fusion(f32[16,128]{1,0:T(8,128)} %get-tuple-element.8), kind=kLoop, calls=%fused_computation.3 | loop fusion | bytes 128 | tf_op jit(solution)/shard_map/slice | solution.py:631
  67.1 1.9 %copy.14 = f32[2,16,16,256]{3,2,1,0:T(8,128)} copy(f32[2,16,16,256]{3,2,1,0:T(8,128)} %bitcast.6) | data formatting | bytes 1048576
  68.9 1.3 %copy.15 = f32[16,256]{1,0:T(8,128)} copy(f32[16,256]{1,0:T(8,128)} %get-tuple-element.13) | data formatting | bytes 32768
Async XLA Ops:
  3.0 1.8 %copy-start = (bf16[1536,16]{0,1:T(8,128)(2,1)S(1)}, bf16[1536,16]{0,1:T(8,128)(2,1)}, u32[]{:S(2)}) copy-start(bf16[1536,16]{0,1:T(8,128)(2,1)} %param.10) | copy-start | bytes 147460
  3.0 1.8 %copy-start.1 = (bf16[1536,16]{0,1:T(8,128)(2,1)S(1)}, bf16[1536,16]{0,1:T(8,128)(2,1)}, u32[]{:S(2)}) copy-start(bf16[1536,16]{0,1:T(8,128)(2,1)} %param.9) | copy-start | bytes 147460

commit v17 on v16

--- a/solution.py
+++ b/solution.py
@@ -526,8 +526,14 @@
         start(vbuf.at[slot], vsend.at[sem + 1], dev(0, -1), slot)
         sem += 2
         compute(slot)
-    for db, relay, lo in [(-1, True, 1), (1, False, 1), (-2, False, 0)]:
-        lax.fori_loop(lo, 4, row_step(db, relay), 0)
+    below = row_step(-1, True)
+    above = row_step(1, False)
+
+    def both_rows(i, carry):
+        return above(i, below(i, carry))
+
+    lax.fori_loop(1, 4, both_rows, 0)
+    lax.fori_loop(0, 4, row_step(-2, False), 0)
 
     span = hist_ref.shape[1]
     mine = pl.ds(pl.multiple_of(core * span, span), span)

time: 70.6 us -> 68.8 us (0.975)
  Pallas kernels: 60.2 us -> 58.4 us
    pallas_call x1, Pallas kernels: 60.2 us -> 58.4 us  [pair_split(): pl.pallas_call(functools.partial(pair_split_kernel, nodes=nodes, targets=...]
where the time goes in v17:
time: 68.8 us; the launch traced here: 68.5 us
  Pallas kernels  58.4 us (85%)
  local copies, waits for them, and re-layouts  6.34 us (9%)
  other arithmetic  3.02 us (4%)
    pallas_call x1, Pallas kernels, pair_split(): pl.pallas_call(functools.partial(pair_split_kernel, nodes=nodes, targets=...  58.4 us
    unnamed x6, local copies, waits for them, and re-layouts  3.2 us
    convert_element_type x1, other arithmetic, local(): seg_t = (codes.T + node_of_row[None, :] * BINS).astype(jnp.int16)  1.67 us

profile of v17, /device:TPU:1, one launch (start us, length us, event | category | flops | bytes accessed | tf_op | source)
XLA Modules:
  0.0 68.5 jit_solution(7665180783264199913)
XLA Ops:
  0.6 0.7 %broadcast_multiply_fusion = s32[1536]{0:T(1024)S(1)} fusion(s32[1536]{0:T(1024)} %param.8), kind=kLoop, calls=%fused_computation.4 | loop fusion | flops 1536 | bytes 12288 | tf_op jit(solution)/shard_map/mul | solution.py:631
  1.3 1.7 %fusion = s16[256,1536]{0,1:T(8,128)(2,1)S(1)} fusion(s32[1536,256]{1,0:T(8,128)} %param.7, s32[1536]{0:T(1024)S(1)} %broadcast_multiply_fusion), kind=kLoop, calls=%fused_computation.1 | loop fusion | flops 786432 | bytes 2365440 | tf_op jit(solution)/shard_map/convert_element_type | solution.py:631
  3.0 0.0 copy-start
  3.0 0.0 copy-start.1
  3.0 0.7 copy.11
  3.7 1.1 %reshape_reshape.3.seg_ref = s16[16,32,768]{2,1,0:T(8,128)(2,1)} reshape(s16[256,1536]{1,0:T(8,128)(2,1)S(1)} %copy.11) | data formatting | bytes 1572864 | tf_op jit(solution)/shard_map/reshape;reshape | solution.py:632
  4.9 0.0 copy-done
  4.9 0.0 copy-done.1
  4.9 0.6 pad_maximum_fusion.v_ref
  5.5 58.4 %shard_map.94 = (f32[512,256]{1,0:T(8,128)}, f32[16,256]{1,0:T(8,128)}, f32[16,128]{1,0:T(8,128)}) custom-call(s32[8]{0:T(128)} %small_ref.1, s32[8]{0:T(128)} %evict_ref.1, s16[16,32,768]{2,1,0:T(8,128)(2,1)} %reshape_reshape.3.seg_ref, bf16[32,1536]{1,0:T(8,128)(2,1)} %pad_maximum_fusion.v_ref, f32[256,256]{1,0:T(8,128)} %bitcast.9), custom_call_target="tpu_custom_call" | custom-call | flops 12884901888 | bytes 5767168 | tf_op jit(solution)/shard_map/pallas_call | solution.py:580
  64.0 1.3 %slice_reduce_fusion = f32[16]{0:T(128)} fusion(f32[16,128]{1,0:T(8,128)} %get-tuple-element.8), kind=kLoop, calls=%fused_computation.3 | loop fusion | bytes 128 | tf_op jit(solution)/shard_map/slice | solution.py:637
  65.3 1.9 %copy.14 = f32[2,16,16,256]{3,2,1,0:T(8,128)} copy(f32[2,16,16,256]{3,2,1,0:T(8,128)} %bitcast.6) | data formatting | bytes 1048576
  67.2 1.3 %copy.15 = f32[16,256]{1,0:T(8,128)} copy(f32[16,256]{1,0:T(8,128)} %get-tuple-element.13) | data formatting | bytes 32768
Async XLA Ops:
  3.0 1.8 %copy-start = (bf16[1536,16]{0,1:T(8,128)(2,1)S(1)}, bf16[1536,16]{0,1:T(8,128)(2,1)}, u32[]{:S(2)}) copy-start(bf16[1536,16]{0,1:T(8,128)(2,1)} %param.10) | copy-start | bytes 147460
  3.0 1.8 %copy-start.1 = (bf16[1536,16]{0,1:T(8,128)(2,1)S(1)}, bf16[1536,16]{0,1:T(8,128)(2,1)}, u32[]{:S(2)}) copy-start(bf16[1536,16]{0,1:T(8,128)(2,1)} %param.9) | copy-start | bytes 147460

commit v18 on v17

--- a/solution.py
+++ b/solution.py
@@ -529,11 +529,13 @@
     below = row_step(-1, True)
     above = row_step(1, False)
 
+    beyond = row_step(-2, False)
+
     def both_rows(i, carry):
-        return above(i, below(i, carry))
+        return beyond(i - 1, above(i, below(i, carry)))
 
     lax.fori_loop(1, 4, both_rows, 0)
-    lax.fori_loop(0, 4, row_step(-2, False), 0)
+    lax.fori_loop(3, 4, beyond, 0)
 
     span = hist_ref.shape[1]
     mine = pl.ds(pl.multiple_of(core * span, span), span)

time: 68.8 us -> 69.9 us (1.016)
  Pallas kernels: 58.4 us -> 59.6 us
    pallas_call x1, Pallas kernels: 58.4 us -> 59.6 us  [pair_split(): pl.pallas_call(functools.partial(pair_split_kernel, nodes=nodes, targets=...]
where the time goes in v18:
time: 69.9 us; the launch traced here: 69.6 us
  Pallas kernels  59.6 us (85%)
  local copies, waits for them, and re-layouts  6.34 us (9%)
  other arithmetic  3.02 us (4%)
    pallas_call x1, Pallas kernels, pair_split(): pl.pallas_call(functools.partial(pair_split_kernel, nodes=nodes, targets=...  59.6 us
    unnamed x6, local copies, waits for them, and re-layouts  3.2 us
    convert_element_type x1, other arithmetic, local(): seg_t = (codes.T + node_of_row[None, :] * BINS).astype(jnp.int16)  1.67 us

profile of v18, /device:TPU:1, one launch (start us, length us, event | category | flops | bytes accessed | tf_op | source)
XLA Modules:
  0.0 69.6 jit_solution(7725713035764966599)
XLA Ops:
  0.6 0.7 %broadcast_multiply_fusion = s32[1536]{0:T(1024)S(1)} fusion(s32[1536]{0:T(1024)} %param.8), kind=kLoop, calls=%fused_computation.4 | loop fusion | flops 1536 | bytes 12288 | tf_op jit(solution)/shard_map/mul | solution.py:633
  1.3 1.7 %fusion = s16[256,1536]{0,1:T(8,128)(2,1)S(1)} fusion(s32[1536,256]{1,0:T(8,128)} %param.7, s32[1536]{0:T(1024)S(1)} %broadcast_multiply_fusion), kind=kLoop, calls=%fused_computation.1 | loop fusion | flops 786432 | bytes 2365440 | tf_op jit(solution)/shard_map/convert_element_type | solution.py:633
  3.0 0.0 copy-start
  3.0 0.0 copy-start.1
  3.0 0.7 copy.11
  3.7 1.1 %reshape_reshape.3.seg_ref = s16[16,32,768]{2,1,0:T(8,128)(2,1)} reshape(s16[256,1536]{1,0:T(8,128)(2,1)S(1)} %copy.11) | data formatting | bytes 1572864 | tf_op jit(solution)/shard_map/reshape;reshape | solution.py:634
  4.9 0.0 copy-done
  4.9 0.0 copy-done.1
  4.9 0.6 pad_maximum_fusion.v_ref
  5.5 59.6 %shard_map.94 = (f32[512,256]{1,0:T(8,128)}, f32[16,256]{1,0:T(8,128)}, f32[16,128]{1,0:T(8,128)}) custom-call(s32[8]{0:T(128)} %small_ref.1, s32[8]{0:T(128)} %evict_ref.1, s16[16,32,768]{2,1,0:T(8,128)(2,1)} %reshape_reshape.3.seg_ref, bf16[32,1536]{1,0:T(8,128)(2,1)} %pad_maximum_fusion.v_ref, f32[256,256]{1,0:T(8,128)} %bitcast.9), custom_call_target="tpu_custom_call" | custom-call | flops 12884901888 | bytes 5767168 | tf_op jit(solution)/shard_map/pallas_call | solution.py:582
  65.1 1.3 %slice_reduce_fusion = f32[16]{0:T(128)} fusion(f32[16,128]{1,0:T(8,128)} %get-tuple-element.8), kind=kLoop, calls=%fused_computation.3 | loop fusion | bytes 128 | tf_op jit(solution)/shard_map/slice | solution.py:639
  66.4 1.9 %copy.14 = f32[2,16,16,256]{3,2,1,0:T(8,128)} copy(f32[2,16,16,256]{3,2,1,0:T(8,128)} %bitcast.6) | data formatting | bytes 1048576
  68.3 1.3 %copy.15 = f32[16,256]{1,0:T(8,128)} copy(f32[16,256]{1,0:T(8,128)} %get-tuple-element.13) | data formatting | bytes 32768
Async XLA Ops:
  3.0 1.8 %copy-start = (bf16[1536,16]{0,1:T(8,128)(2,1)S(1)}, bf16[1536,16]{0,1:T(8,128)(2,1)}, u32[]{:S(2)}) copy-start(bf16[1536,16]{0,1:T(8,128)(2,1)} %param.10) | copy-start | bytes 147460
  3.0 1.8 %copy-start.1 = (bf16[1536,16]{0,1:T(8,128)(2,1)S(1)}, bf16[1536,16]{0,1:T(8,128)(2,1)}, u32[]{:S(2)}) copy-start(bf16[1536,16]{0,1:T(8,128)(2,1)} %param.9) | copy-start | bytes 147460

commit v19 on v17

--- a/solution.py
+++ b/solution.py
@@ -512,11 +512,8 @@
         return body
 
     sem = 4
-    for da in [-1, 1, None, -2]:
-        if da is None:
-            for db, relay in [(-1, True), (1, False)]:
-                lax.fori_loop(0, 1, row_step(db, relay), 0)
-            continue
+
+    def first_axis(da, sem):
         slot = dev(da, 0)
         arrive(slot)
         if da == -1:
@@ -524,15 +521,22 @@
             sem += 1
         start(vbuf.at[slot], vsend.at[sem], dev(0, 1), slot)
         start(vbuf.at[slot], vsend.at[sem + 1], dev(0, -1), slot)
-        sem += 2
         compute(slot)
+        return sem + 2
+
+    for da in [-1, 1]:
+        sem = first_axis(da, sem)
     below = row_step(-1, True)
     above = row_step(1, False)
+    lax.fori_loop(0, 1, below, 0)
+    lax.fori_loop(0, 1, above, 0)
 
     def both_rows(i, carry):
         return above(i, below(i, carry))
 
-    lax.fori_loop(1, 4, both_rows, 0)
+    lax.fori_loop(1, 2, both_rows, 0)
+    sem = first_axis(-2, sem)
+    lax.fori_loop(2, 4, both_rows, 0)
     lax.fori_loop(0, 4, row_step(-2, False), 0)
 
     span = hist_ref.shape[1]

time: 68.8 us -> 69.2 us (level); the launches traced: 68.5 us -> 68.2 us
  no operation moved by 1% of the time
where the time goes in v19:
time: 69.2 us; the launch traced here: 68.2 us
  Pallas kernels  58.1 us (84%)
  local copies, waits for them, and re-layouts  6.34 us (9%)
  other arithmetic  3.02 us (4%)
    pallas_call x1, Pallas kernels, pair_split(): pl.pallas_call(functools.partial(pair_split_kernel, nodes=nodes, targets=...  58.1 us
    unnamed x6, local copies, waits for them, and re-layouts  3.2 us
    convert_element_type x1, other arithmetic, local(): seg_t = (codes.T + node_of_row[None, :] * BINS).astype(jnp.int16)  1.67 us

profile of v19, /device:TPU:1, one launch (start us, length us, event | category | flops | bytes accessed | tf_op | source)
XLA Modules:
  0.0 68.2 jit_solution(13120567921854711453)
XLA Ops:
  0.6 0.7 %broadcast_multiply_fusion = s32[1536]{0:T(1024)S(1)} fusion(s32[1536]{0:T(1024)} %param.8), kind=kLoop, calls=%fused_computation.4 | loop fusion | flops 1536 | bytes 12288 | tf_op jit(solution)/shard_map/mul | solution.py:635
  1.3 1.7 %fusion = s16[256,1536]{0,1:T(8,128)(2,1)S(1)} fusion(s32[1536,256]{1,0:T(8,128)} %param.7, s32[1536]{0:T(1024)S(1)} %broadcast_multiply_fusion), kind=kLoop, calls=%fused_computation.1 | loop fusion | flops 786432 | bytes 2365440 | tf_op jit(solution)/shard_map/convert_element_type | solution.py:635
  3.0 0.0 copy-start
  3.0 0.0 copy-start.1
  3.0 0.7 copy.11
  3.7 1.1 %reshape_reshape.3.seg_ref = s16[16,32,768]{2,1,0:T(8,128)(2,1)} reshape(s16[256,1536]{1,0:T(8,128)(2,1)S(1)} %copy.11) | data formatting | bytes 1572864 | tf_op jit(solution)/shard_map/reshape;reshape | solution.py:636
  4.9 0.0 copy-done
  4.9 0.0 copy-done.1
  4.9 0.6 pad_maximum_fusion.v_ref
  5.5 58.1 %shard_map.94 = (f32[512,256]{1,0:T(8,128)}, f32[16,256]{1,0:T(8,128)}, f32[16,128]{1,0:T(8,128)}) custom-call(s32[8]{0:T(128)} %small_ref.1, s32[8]{0:T(128)} %evict_ref.1, s16[16,32,768]{2,1,0:T(8,128)(2,1)} %reshape_reshape.3.seg_ref, bf16[32,1536]{1,0:T(8,128)(2,1)} %pad_maximum_fusion.v_ref, f32[256,256]{1,0:T(8,128)} %bitcast.9), custom_call_target="tpu_custom_call" | custom-call | flops 12884901888 | bytes 5767168 | tf_op jit(solution)/shard_map/pallas_call | solution.py:584
  63.7 1.3 %slice_reduce_fusion = f32[16]{0:T(128)} fusion(f32[16,128]{1,0:T(8,128)} %get-tuple-element.8), kind=kLoop, calls=%fused_computation.3 | loop fusion | bytes 128 | tf_op jit(solution)/shard_map/slice | solution.py:641
  65.0 1.9 %copy.14 = f32[2,16,16,256]{3,2,1,0:T(8,128)} copy(f32[2,16,16,256]{3,2,1,0:T(8,128)} %bitcast.6) | data formatting | bytes 1048576
  66.9 1.3 %copy.15 = f32[16,256]{1,0:T(8,128)} copy(f32[16,256]{1,0:T(8,128)} %get-tuple-element.13) | data formatting | bytes 32768
Async XLA Ops:
  3.0 1.8 %copy-start = (bf16[1536,16]{0,1:T(8,128)(2,1)S(1)}, bf16[1536,16]{0,1:T(8,128)(2,1)}, u32[]{:S(2)}) copy-start(bf16[1536,16]{0,1:T(8,128)(2,1)} %param.10) | copy-start | bytes 147460
  3.0 1.8 %copy-start.1 = (bf16[1536,16]{0,1:T(8,128)(2,1)S(1)}, bf16[1536,16]{0,1:T(8,128)(2,1)}, u32[]{:S(2)}) copy-start(bf16[1536,16]{0,1:T(8,128)(2,1)} %param.9) | copy-start | bytes 147460
